TPU v7x, 128 devices: a whole 4x4x4 slice. The times are simulated.
128 devices in a mesh: row: 8 (over z, x_hi), col: 16 (over y, x_lo, core).
Axes of the slice: x: 4 (x_hi: 2, x_lo: 2; x = x_hi * 2 + x_lo), y: 4, z: 4, core: 2. Of those that a mesh axis runs over, the one named last changes fastest.
Arguments:
- trailing: float32 [16384, 16384], P('row', 'col'), may hold values from -6 to 6
- panel_factors: float32 [2048, 16384], P('col', 'row'), may hold values from -1.2 to 1.2
- vectors_t: float32 [32, 64, 512], P('col'), may hold values from -0.25 to 0.25
- inverse_lower_factors: float32 [32, 512, 512], P('col', 'row'), as said below
- slot_of_panel: int32 [32], replicated, may hold values from 0 to 31, each once
Outputs:
- updated: float32 [16384, 16384], P('row', 'col')
Inputs may be any that keep to these rules, and one draw needn't show every extreme that they name: `slot_of_panel`: a permutation of the panels' slots. `inverse_lower_factors`: each slot's matrix is lower triangular with a positive diagonal.
All inputs are finite; a program needn't handle non-finite values.
Results may differ from a plain program's by a relative error of at most 0.000075.
Values sent between devices are 32-bit elements; how exact they have to be, the bound alone decides.
A program may use at most 256 MiB of HBM per device.

v0:
```python
import jax
import jax.numpy as jnp
from jax import lax
from jax.sharding import PartitionSpec as P


def copy_for_each(shard, axis):
    copies = jnp.broadcast_to(shard, (lax.axis_size(axis), *shard.shape))
    return lax.all_to_all(copies, axis, split_axis=0, concat_axis=0, tiled=True)


def over_copies(shard, axis):
    everything = copy_for_each(shard, axis)
    return jnp.sum(everything, axis=0)


def joined_along(parts, dim):
    parts = jnp.moveaxis(parts, 0, dim)
    shape = parts.shape
    return parts.reshape(*shape[:dim], shape[dim] * shape[dim + 1], *shape[dim + 2 :])


def gather_directly(shard, axis, dim):
    return joined_along(copy_for_each(shard, axis), dim)


def body(trailing, panel_factors, vectors_t, inverse_lower_factors, slot_of_panel):
    highest_precision = lax.Precision.HIGHEST
    per_col = vectors_t.shape[0]
    rank = vectors_t.shape[1]
    panels = per_col * lax.axis_size("col")
    rows_blk = trailing.shape[0]
    solved_panel = lax.dot_general(
        vectors_t, inverse_lower_factors, (((2,), (2,)), ((0,), (0,))), precision=highest_precision
    )
    partial_core_block = jnp.einsum(
        "fdv,fpv->fdp", solved_panel, solved_panel, precision=highest_precision
    )
    summed = over_copies(partial_core_block, "row")
    core_blocks = gather_directly(summed, "col", 0)
    onehot = (slot_of_panel[:, None] == jnp.arange(panels, dtype=jnp.int32)[None, :]).astype(
        jnp.float32
    )
    panel_cores = jnp.dot(
        onehot, core_blocks.reshape(panels, rank * rank), precision=highest_precision
    ).reshape(panels, rank, rank)
    tall = lax.all_gather(panel_factors, "row", axis=1, tiled=True)
    column_factor = lax.all_to_all(tall, "col", split_axis=1, concat_axis=0, tiled=True)
    piece = lax.all_gather(panel_factors, "col", axis=0, tiled=True)
    width = piece.shape[0]
    count = width // rank
    scaled = jnp.einsum(
        "pab,pbi->pai",
        panel_cores,
        piece.reshape(count, rank, rows_blk),
        precision=highest_precision,
    )
    update = lax.dot_general(
        scaled.reshape(width, rows_blk),
        column_factor,
        (((0,), (0,)), ((), ())),
        precision=highest_precision,
    )
    return trailing - update


def solution(mesh):
    return jax.shard_map(
        body,
        mesh=mesh,
        in_specs=(
            P("row", "col"),
            P("col", "row"),
            P("col", None, None),
            P("col", "row", None),
            P(),
        ),
        out_specs=P("row", "col"),
        check_vma=False,
    )
```

profile of v0, /device:TPU:26, one launch (start us, length us, event | category | flops | bytes accessed | tf_op | source)
XLA Modules:
  0.0 390.3 jit_solution(3864483176128176112)
XLA Ops:
  6.5 0.0 copy-start
  6.5 0.0 all-gather.5.cloned.1.call-start
  6.5 2.6 copy.15
  9.1 0.0 all-gather.5.cloned.1.call-update
  9.1 0.0 all-gather.3.cloned.1.call-start
  9.2 0.7 all-gather.3.cloned.1.call-update
  9.9 0.0 copy-done
  9.9 1.3 fusion.7
  11.2 0.2 fusion.8
  11.5 0.3 reshape.15
  11.8 15.5 %all_to_all.29 = f32[8,1,8192]{2,1,0:T(1,128)S(1)} all-to-all(f32[8,1,8192]{2,1,0:T(1,128)S(1)} %reshape.15), channel_id=1, replica_groups=mesh['row'=8,'col'=16] {'row'}, dimensions={0} | all-to-all | bytes 524288 | tf_op jit(solution)/shard_map/all_to_all | solution.py:9
  27.3 0.5 broadcast.1
  27.9 1.2 reduce
  29.0 0.2 reshape.16
  29.3 0.1 broadcast_in_dim.9
  29.4 0.7 reshape.17
  30.1 12.8 %all_to_all.30 = f32[16,1,8192]{2,1,0:T(1,128)S(1)} all-to-all(f32[16,1,8192]{2,1,0:T(1,128)S(1)} %reshape.17), channel_id=1, replica_groups=mesh['row'=8,'col'=16] {'col'}, dimensions={0} | all-to-all | bytes 1048576 | tf_op jit(solution)/shard_map/all_to_all | solution.py:9
  42.8 75.1 %all-gather.5.cloned.1.call-done = f32[128,16384]{0,1:T(8,128)} async-done(((f32[128,2048]{0,1:T(8,128)}), f32[128,16384]{0,1:T(8,128)}) %all-gather.5.cloned.1.call-update) | async-done | bytes 8388624 | tf_op jit(solution)/shard_map/all_gather | solution.py:47
  117.9 6.1 %all-to-all-start.2 = ((f32[128,16,1024]{0,2,1:T(8,128)}), f32[128,16,1024]{0,2,1:T(8,128)}, u32[]{:S(2)}, u32[]{:S(2)}) async-start(f32[128,16,1024]{0,2,1:T(8,128)} %bitcast.22), calls=%async_computation.2 | async-start | bytes 16777216 | tf_op jit(solution)/shard_map/all_to_all | solution.py:48
  124.1 1.8 reduce.1
  125.9 0.4 reshape.18
  126.3 0.4 reshape_reshape.3
  126.6 0.4 dot_general.22
  127.1 0.0 copy-done.3
  127.1 1.3 fusion.2
  128.4 155.8 %all-to-all-done.2 = f32[128,16,1024]{0,2,1:T(8,128)} async-done(((f32[128,16,1024]{0,2,1:T(8,128)}), f32[128,16,1024]{0,2,1:T(8,128)}, u32[]{:S(2)}, u32[]{:S(2)}) %all-to-all-start.2) | async-done | bytes 8388640 | tf_op jit(solution)/shard_map/all_to_all | solution.py:48
  284.1 9.3 %copy.16 = f32[16,128,1024]{2,1,0:T(8,128)} copy(f32[16,128,1024]{1,2,0:T(8,128)} %bitcast.5) | data formatting | bytes 16777216 | tf_op jit(solution)/shard_map/all_to_all | solution.py:48
  293.4 9.6 %all-gather.3.cloned.1.call-done = f32[2048,2048]{1,0:T(8,128)} async-done(((f32[128,2048]{1,0:T(8,128)}), f32[2048,2048]{1,0:T(8,128)}) %all-gather.3.cloned.1.call-update) | async-done | bytes 16777232 | tf_op jit(solution)/shard_map/all_gather | solution.py:49
  303.1 22.2 %fusion = f32[32,64,2048]{2,1,0:T(8,128)} fusion(f32[32,64,2048]{2,1,0:T(8,128)} %bitcast.20, f32[32,64,64]{2,0,1:T(8,128)S(1)} %fusion.2), kind=kOutput, calls=%fused_computation.1 | convolution fusion | flops 3221225472 | bytes 34078720 | tf_op jit(solution)/shard_map/pab,pbi->pai/dot_general | solution.py:52
  325.2 0.0 copy-done.2
  325.2 58.2 %convolution_subtract_fusion = f32[2048,1024]{1,0:T(8,128)} fusion(f32[2048,1024]{1,0:T(8,128)} %param.5, f32[2048,2048]{1,0:T(8,128)} %bitcast.21, f32[2048,1024]{1,0:T(8,128)S(1)} %bitcast.23), kind=kOutput, calls=%fused_computation | convolution fusion | flops 51541704704 | bytes 41943040 | tf_op jit(solution)/shard_map/dot_general | solution.py:58
  383.4 0.0 copy-done.1
  (5 shorter events, 0.1 us)
Async XLA Ops:
  6.5 3.4 copy-start
  6.5 111.4 %all-gather.5.cloned.1.call-start = ((), (), s32[]{:S(2)}) async-start(), calls=%async_computation.4 | async-start | bytes 9437184 | tf_op jit(solution)/shard_map/all_gather | solution.py:47
  9.1 293.9 %all-gather.3.cloned.1.call-start = ((), (), s32[]{:S(2)}) async-start(), calls=%async_computation.3 | async-start | bytes 17825792 | tf_op jit(solution)/shard_map/all_gather | solution.py:49
  117.9 9.1 %copy-start.3 = (s32[32]{0:T(128)S(1)}, s32[32]{0:T(128)}, u32[]{:S(2)}) copy-start(s32[32]{0:T(128)} %param.9) | copy-start | bytes 388
  117.9 166.2 %all-to-all-start.2 = ((f32[128,16,1024]{0,2,1:T(8,128)}), f32[128,16,1024]{0,2,1:T(8,128)}, u32[]{:S(2)}, u32[]{:S(2)}) async-start(f32[128,16,1024]{0,2,1:T(8,128)} %bitcast.22), calls=%async_computation.2 | async-start | bytes 16777216 | tf_op jit(solution)/shard_map/all_to_all | solution.py:48
  303.1 22.2 %copy-start.2 = (f32[16,128,1024]{2,1,0:T(8,128)S(1)}, f32[16,128,1024]{2,1,0:T(8,128)}, u32[]{:S(2)}) copy-start(f32[16,128,1024]{2,1,0:T(8,128)} %copy.16) | copy-start | bytes 25165828
  325.2 58.2 %copy-start.1 = (f32[2,64,512]{2,1,0:T(8,128)S(1)}, f32[2,64,512]{2,1,0:T(8,128)}, u32[]{:S(2)}) copy-start(f32[2,64,512]{2,1,0:T(8,128)} %param.7) | copy-start | bytes 786436
Sparse Core Ops, SparseCore 0:
  9.7 108.1 all-gather.4
  119.6 183.3 all-gather.2
where the time goes:
time: 394 us; the launch traced here: 390 us
  waiting for transfers between devices  241 us (61%)
  matrix products  83.2 us (21%)
  blocking collectives  28.2 us (7%)
  local copies, waits for them, and re-layouts  14.9 us (4%)
  between operations  13.5 us (3%)
  starting transfers between devices  6.17 us (2%)
    all_to_all x1, waiting for transfers between devices, body(): lax.all_to_all(tall, 'col', split_axis=1, concat_axis=0, tiled=True)  156 us
    all_gather x1, waiting for transfers between devices, body(): tall = lax.all_gather(panel_factors, 'row', axis=1, tiled=True)  75.1 us
    dot_general x1, matrix products, body(): lax.dot_general(scaled.reshape(width, rows_blk), column_factor, (((0,), (...  58.2 us
    all_to_all x2, blocking collectives, copy_for_each(): return lax.all_to_all(copies, axis, split_axis=0, concat_axis=0, tiled=True)  28.2 us
    dot_general x1, matrix products, body(): jnp.einsum('pab,pbi->pai', panel_cores, piece.reshape(count, rank, rows_b...  22.2 us
    all_gather x1, waiting for transfers between devices, body(): piece = lax.all_gather(panel_factors, 'col', axis=0, tiled=True)  9.63 us
    all_to_all x1, local copies, waits for them, and re-layouts, body(): lax.all_to_all(tall, 'col', split_axis=1, concat_axis=0, tiled=True)  9.31 us
  transfers between devices with their start and end apart: 3, of which 3 were waited for; matrix products, arithmetic and copies ran while one was open for 5% of the time, Pallas kernels for 0%

commit v1 on v0

v1 whole, which is shorter than its diff:
```python
import jax
import jax.numpy as jnp
from jax import lax
from jax.experimental import pallas as pl
from jax.experimental.pallas import tpu as pltpu
from jax.sharding import PartitionSpec as P

MESH = pl.DeviceIdType.MESH
F32, BF16, I32 = jnp.float32, jnp.bfloat16, jnp.int32

ITEMS = (
    (16, 24720, 57394, 81938, 262224, 73745, 20785, 434192),
    (438273, 397332, 94864, 16435, 16497, 86482, 57362, 430224),
    (57346, 28674, 24947, 28672, 12386, 33219, 69747, 127106),
    (262196, 62034, 8210, 53554, 77875, 401412, 36865, 98387),
    (16464, 119363, 4240, 393717, 408659, 110641, 115538, 12417),
    (65571, 176710, 41138, 20946, 284692, 422672, 8881, 355666),
    (262181, 8656, 4259, 160198, 131094, 8402, 193190, 412997),
    (90768, 115138, 393349, 440337, 360720, 151750, 103154, 53714),
    (316037, 418244, 163974, 264196, 33025, 405620, 53987, 20723),
    (201350, 147910, 151718, 86544, 65795, 135270, 49937, 238022),
    (330803, 28883, 119026, 90627, 91122, 426544, 66307, 159974),
    (287156, 155846, 250086, 184838, 414693, 418341, 226022, 418416),
    (180646, 428049, 127328, 24690, 258310, 156198, 164614, 115297),
    (273776, 74610, 2071, 12387, 164838, 371955, 119074, 45667),
    (41106, 217958, 28978, 139366, 4195, 416996, 24674, 152166),
    (355346, 86147, 33059, 36944, 266384, 61475, 425168, 351538),
    (147590, 293301, 168230, 151622, 41090, 53330, 45138, 351344),
    (269523, 32898, 94850, 396307, 32899, 143430, 135238, 298081),
    (16387, 49683, 78322, 41874, 147590, 273584, 86195, 426896),
    (242614, 265488, 184806, 86915, 326802, 335009, 147622, 21378),
    (78000, 426036, 221910, 422789, 412787, 41395, 20530, 250758),
    (450721, 172070, 272629, 177030, 2775, 233894, 32803, 36930),
    (151718, 24914, 143446, 334036, 277268, 384275, 139302, 61571),
    (8466, 164166, 404016, 420369, 301829, 13009, 20851, 415921),
    (20739, 58163, 371236, 265584, 2903, 197318, 176486, 293028),
    (315652, 160022, 20483, 317716, 36929, 25346, 411889, 41651),
    (266501, 424657, 246678, 94499, 326835, 49681, 288996, 193190),
    (155910, 387781, 139382, 430421, 393941, 205318, 376051, 281810),
    (376050, 272949, 2487, 135494, 205510, 164182, 50162, 425157),
    (332020, 69635, 205206, 269520, 287152, 264213, 78819, 221718),
    (159974, 276533, 393812, 61922, 45473, 272469, 259046, 185142),
    (164054, 151670, 180806, 436273, 184742, 2359, 184758, 438576),
    (294352, 28672, 101396, 268324, 359666, 407761, 102497, 24866),
    (285971, 2903, 400389, 277681, 272436, 213686, 217590, 147750),
    (168246, 143446, 280628, 402357, 268325, 403953, 45347, 82643),
    (277810, 16560, 437201, 193446, 377328, 281061, 298064, 285364),
    (98992, 94371, 285841, 2487, 102881, 277520, 400452, 338597),
    (279204, 139430, 74002, 2135, 168422, 400389, 280756, 268404),
    (291493, 254358, 147718, 305716, 53315, 16626, 110801, 45058),
    (209574, 347376, 217782, 12432, 305844, 159974, 213190, 413744),
    (45394, 123682, 420177, 188550, 2135, 126004, 172374, 57379),
    (172358, 273521, 358724, 281936, 282960, 176406, 2071, 143398),
    (285778, 400402, 24930, 164086, 172358, 2807, 66193, 422832),
    (340340, 404338, 2135, 66290, 2647, 411793, 127619, 29602),
    (340325, 306257, 290128, 414437, 346324, 2103, 156294, 177062),
    (176486, 432369, 90930, 217830, 350405, 309364, 58177, 403472),
    (49264, 280805, 123683, 77858, 74289, 168086, 2103, 276485),
    (7, 205590, 234278, 118787, 2167, 7, 284948, 306450),
    (7, 2135, 32978, 2167, 7, 7, 289029, 428083),
    (7, 419952, 155846, 7, 7, 7, 2135, 318834),
    (7, 415841, 2167, 7, 7, 7, 188886, 433507),
    (7, 325973, 7, 7, 7, 7, 106499, 276564),
    (7, 74528, 7, 7, 7, 7, 151702, 66242),
    (7, 2199, 7, 7, 7, 7, 2167, 172310),
    (7, 7, 7, 7, 7, 7, 301205, 110802),
    (7, 7, 7, 7, 7, 7, 7, 200902),
    (7, 7, 7, 7, 7, 7, 7, 421045),
    (7, 7, 7, 7, 7, 7, 7, 294032),
    (7, 7, 7, 7, 7, 7, 7, 310401),
    (7, 7, 7, 7, 7, 7, 7, 139382),
    (7, 7, 7, 7, 7, 7, 7, 411985),
    (7, 7, 7, 7, 7, 7, 7, 164214),
    (446865, 2679, 115440, 143542, 37490, 209078, 396560, 343282),
    (344452, 434548, 94947, 107120, 41571, 28977, 433412, 7),
    (287109, 246118, 201446, 209510, 209510, 28962, 7, 7),
    (184710, 298129, 2199, 298035, 90289, 393508, 7, 7),
    (119282, 310576, 7, 2199, 151718, 172326, 7, 7),
    (188902, 2807, 7, 7, 297876, 32802, 7, 7),
    (106562, 7, 7, 7, 7, 7, 7, 7),
    (230198, 7, 7, 7, 7, 7, 7, 7),
    (384178, 222166, 7, 7, 2999, 2743, 52528, 7),
    (7, 7, 7, 7, 122946, 7, 330800, 7),
    (299076, 2231, 127858, 229974, 385328, 301236, 7, 60501),
    (7, 407763, 37731, 7, 98593, 94211, 7, 334324),
    (7, 358597, 197478, 7, 192806, 330388, 7, 301204),
    (7, 7, 2231, 7, 7, 7, 7, 305812),
    (7, 7, 426961, 7, 7, 7, 7, 49857),
    (7, 7, 238534, 7, 7, 7, 7, 7),
    (106960, 408757, 62387, 407729, 2295, 420721, 416305, 86194),
    (360900, 188662, 160678, 289396, 294098, 355173, 317988, 155814),
    (192966, 103344, 293365, 155862, 246742, 70609, 159990, 45057),
    (197142, 410532, 2263, 301428, 2199, 185286, 2263, 2263),
    (7, 242598, 7, 306321, 2231, 298192, 127890, 2295),
    (7, 7, 7, 310384, 409813, 180854, 111491, 7),
    (7, 7, 7, 254678, 155846, 314512, 234374, 7),
    (7, 7, 7, 2711, 321908, 326785, 74002, 7),
    (7, 7, 7, 127827, 295696, 82691, 229638, 7),
    (7, 7, 7, 213830, 217862, 250230, 321844, 7),
    (7, 7, 7, 123282, 49522, 321780, 7, 7),
    (7, 7, 7, 168326, 225638, 313573, 7, 7),
    (7, 7, 7, 172310, 314324, 65538, 7, 7),
    (7, 7, 7, 309556, 306117, 123474, 7, 7),
    (7, 7, 7, 2295, 311840, 201286, 7, 7),
    (7, 7, 7, 7, 106737, 7, 7, 7),
    (7, 7, 7, 7, 159974, 7, 7, 7),
    (7, 7, 7, 7, 188886, 7, 7, 7),
    (7, 7, 7, 7, 396307, 7, 7, 7),
    (7, 7, 7, 7, 332176, 7, 7, 7),
    (7, 7, 7, 7, 115074, 7, 7, 7),
    (7, 7, 7, 7, 61827, 7, 7, 7),
    (7, 7, 7, 7, 180614, 7, 7, 7),
    (7, 7, 7, 7, 317716, 7, 7, 7),
    (327088, 201462, 310480, 424721, 98851, 2327, 180630, 379156),
    (53282, 7, 127507, 371460, 176886, 339250, 359125, 53681),
    (82514, 7, 242182, 2391, 366933, 254966, 242550, 111011),
    (107075, 7, 400436, 7, 2359, 321941, 7, 254374),
    (311876, 7, 125989, 7, 7, 2391, 7, 181078),
    (299589, 7, 432401, 7, 7, 7, 7, 2359),
    (205382, 7, 321796, 7, 7, 7, 7, 209302),
    (7, 7, 321797, 7, 7, 7, 7, 7),
    (7, 7, 338228, 7, 7, 7, 7, 7),
    (7, 2359, 86659, 7, 344912, 326005, 7, 7),
    (7, 41810, 7, 7, 234310, 7, 7, 7),
    (7, 213830, 7, 7, 2583, 7, 7, 7),
    (74288, 314577, 2807, 110962, 7, 78225, 7, 7),
    (442913, 2327, 404565, 53603, 7, 237958, 7, 7),
    (213542, 7, 7, 205158, 7, 7, 7, 7),
    (217718, 7, 7, 259062, 7, 7, 7, 7),
    (323684, 180534, 429330, 181206, 334228, 70450, 330100, 2519),
    (221910, 314418, 102866, 2743, 338309, 242470, 338277, 397653),
    (7, 363445, 115139, 321940, 7, 189270, 2391, 168262),
    (7, 184886, 188870, 363760, 7, 7, 111570, 366996),
    (7, 70146, 318576, 7, 7, 7, 201670, 73731),
    (7, 338293, 343137, 7, 7, 7, 7, 2423),
    (7, 250358, 259062, 7, 7, 7, 7, 7),
    (7, 350613, 351060, 7, 7, 7, 7, 7),
    (7, 7, 90448, 7, 7, 7, 7, 7),
    (7, 7, 172358, 7, 7, 7, 7, 7),
    (7, 7, 351536, 7, 7, 7, 7, 7),
    (7, 7, 330929, 7, 7, 7, 7, 7),
    (7, 7, 2423, 7, 7, 7, 7, 7),
    (226038, 61872, 7, 70112, 115345, 2487, 2583, 330768),
    (351571, 197030, 7, 7, 123523, 342837, 119619, 338945),
    (7, 2519, 7, 7, 197254, 2519, 2455, 7),
    (7, 354805, 7, 7, 408626, 7, 7, 7),
    (7, 7, 7, 7, 2487, 7, 7, 7),
    (7, 7, 7, 7, 342516, 7, 7, 7),
    (7, 7, 7, 7, 334309, 7, 7, 7),
    (7, 7, 7, 7, 2519, 7, 7, 7),
    (72820, 94720, 387476, 78259, 365072, 193430, 197206, 7),
    (7, 7, 379269, 201126, 213510, 7, 342932, 7),
    (7, 7, 2679, 7, 354868, 7, 7, 7),
    (7, 7, 7, 7, 363045, 7, 7, 7),
    (359824, 259062, 192950, 432881, 7, 226166, 85013, 2487),
    (7, 2583, 424721, 346612, 7, 7, 7, 7),
    (7, 7, 375557, 2519, 7, 7, 7, 7),
    (353044, 7, 2519, 113937, 127857, 2647, 205334, 197206),
    (307973, 7, 209526, 7, 242534, 355440, 408144, 78323),
    (234246, 7, 379412, 7, 7, 363617, 371268, 246246),
    (7, 7, 371205, 7, 7, 217590, 2487, 2807),
    (7, 7, 225846, 7, 7, 246710, 371157, 226294),
    (7, 7, 7, 7, 7, 404016, 2871, 346900),
    (7, 7, 7, 7, 7, 363045, 2551, 358964),
    (359571, 238230, 2647, 246582, 221782, 2583, 107057, 86081),
    (98403, 209526, 7, 7, 82466, 230038, 254502, 2583),
    (327749, 2647, 7, 7, 2679, 2679, 221910, 119571),
    (7, 225974, 7, 7, 7, 7, 209526, 213766),
    (7, 7, 7, 99091, 2711, 375509, 7, 234358),
    (7, 7, 7, 221958, 7, 258806, 7, 7),
    (7, 7, 7, 367699, 7, 7, 7, 7),
    (7, 7, 7, 94768, 7, 7, 7, 7),
    (7, 7, 7, 225830, 7, 7, 7, 7),
    (238422, 2711, 7, 2647, 230070, 7, 412272, 102962),
    (365524, 2743, 7, 7, 7, 7, 375397, 205350),
    (345029, 234390, 7, 7, 7, 7, 383636, 399952),
    (246726, 7, 7, 7, 7, 7, 7, 375365),
    (7, 230102, 2711, 380208, 7, 371477, 387764, 259030),
    (7, 7, 7, 7, 7, 7, 383653, 2679),
    (7, 7, 7, 7, 7, 7, 250806, 217750),
    (81987, 379669, 230166, 238230, 2807, 117844, 384113, 7),
    (7, 7, 387765, 242358, 367412, 2903, 7, 7),
    (7, 7, 383701, 2775, 379685, 7, 7, 7),
    (364645, 2871, 416560, 7, 7, 7, 7, 7),
    (250742, 7, 7, 250742, 7, 2967, 2807, 2775),
    (90210, 7, 7, 375604, 7, 7, 7, 103155),
    (7, 7, 7, 7, 7, 7, 7, 242406),
    (7, 7, 7, 7, 7, 7, 7, 387892),
    (254870, 2967, 254806, 7, 238390, 2999, 2839, 2903),
    (7, 7, 384240, 7, 7, 7, 392337, 121909),
    (7, 7, 7, 7, 7, 7, 7, 2935),
    (7, 7, 7, 7, 7, 7, 7, 2967),
    (7, 7, 7, 2903, 7, 7, 7, 7),
    (7, 3031, 2935, 2935, 2935, 392148, 246582, 7),
    (7, 7, 7, 7, 7, 7, 2903, 7),
    (7, 7, 7, 7, 7, 7, 2935, 7),
    (259062, 7, 2967, 2967, 7, 7, 392368, 7),
    (7, 7, 2999, 7, 7, 7, 7, 7),
    (7, 7, 7, 7, 7, 7, 7, 2999),
    (7, 7, 392180, 7, 7, 7, 7, 7),
    (7, 7, 392165, 7, 7, 7, 7, 7),
    (7, 3063, 7, 2999, 254870, 3063, 392116, 3031),
    (7, 7, 7, 3031, 250806, 7, 388005, 3063),
    (7, 7, 7, 3063, 3063, 7, 3031, 7),
    (7, 7, 7, 7, 7, 7, 392181, 7),
)
SEGMENTS = (62, 8, 2, 6, 24, 9, 3, 4, 13, 8, 4, 3, 7, 4, 5, 4, 3, 3, 1, 0, 4, 2, 2, 1, 3, 2, 1, 2, 4, 0, 0, 0, 0)
BLOCKS = (
    (803072, 234697, 234570, 239723, 397952, 393901, 722030, 23951),
    (597068, 84289, 307395, 477344, 207824, 296586, 95593, 383079),
    (479365, 668590, 606657, 498284, 518885, 213059, 663765, 35152),
    (910961, 360727, 457207, 886943, 696792, 268111, 241674, 800914),
    (127290, 504977, 153151, 427560, 75679, 616151, 802669, 677733),
    (358443, 648028, 631450, 875248, 437373, 564604, 868543, 589065),
    (498359, 705315, 978648, 848856, 747361, 637821, 162359, 833372),
    (753085, 1039230, 943456, 972084, 249425, 1020888, 616339, 652510),
)
OWN = ((0, 4, 1, 1, 2, 14, 9, 4), (1, 0, 0, 0, 3, 0, 0, 0), (2, 16, 11, 9, 1, 1, 3, 2), (3, 25, 20, 15, 17, 24, 26, 22))
PARTNERS = ((0, 1, 1, 4, 2, 4, 9, 14), (1, 0, 0, 0, 3, 0, 0, 0), (2, 9, 11, 16, 1, 2, 3, 1), (3, 15, 20, 25, 17, 22, 26, 24))
MARKS = (10, 16, 19, 25, 32)
TRANSIT = 15
TI = 512

ROWS, COLS, RANK, HALF = 2048, 1024, 64, 1024
OTHER, COL_SLOT, TRANSIT_SLOT = 32, 64, 96
SLOTS = TRANSIT_SLOT + TRANSIT
NI = len(ITEMS)


def split(x):
    high = x.astype(BF16)
    return high, (x - high.astype(F32)).astype(BF16)


def kernel(
    trailing, factors, vectors, inverse, slots, out,
    acc, buf, right, wide, block_core, part, by_row, total, cores, known, table,
    local_sem, recv_sem, send_sem, own_send, row_send, row_recv, col_send, col_recv, out_sem,
):
    r, c = lax.axis_index("row"), lax.axis_index("col")
    z, x, y, k = r // 2, (r % 2) * 2 + (c // 2) % 2, c // 4, c % 2
    flip = x // 2
    sx, sy = 1 - 2 * flip, 1 - 2 * k
    xc = x + flip * (3 - 2 * x)
    delta = (sy * (y - z) + 4) % 4
    kind = xc * 4 + delta
    diagonal = jnp.where(kind == 0, 1, 0)
    q = c // 2

    def device(x, y, z, k):
        return (z * 2 + x // 2, y * 4 + (x % 2) * 2 + k)

    partner = (r, q * 2 + 1 - k)
    row_peers = [((r + i) % 8, c) for i in range(1, 8)]
    col_peers = [(r, (c + 2 * i) % 16) for i in range(1, 8)]
    outer = device(3 - x, y, z, k)

    start_acc = pltpu.make_async_copy(trailing, acc, local_sem.at[4])
    start_acc.start()
    bits = [kind % 2 == 1, (kind // 2) % 2 == 1, kind // 4 == 1]

    def pick(row):
        pairs = [jnp.where(bits[0], I32(row[2 * a + 1]), I32(row[2 * a])) for a in range(4)]
        pairs = [jnp.where(bits[1], pairs[2 * a + 1], pairs[2 * a]) for a in range(2)]
        return jnp.where(bits[2], pairs[1], pairs[0])

    own = []
    for j in range(2):
        here = jnp.where(k == 0, pick(OWN[j]), pick(OWN[2 + j]))
        there = jnp.where(k == 0, pick(PARTNERS[j]), pick(PARTNERS[2 + j]))
        for h in range(2):
            src = factors.at[pl.ds(j * RANK, RANK), pl.ds(h * HALF, HALF)]
            other = jnp.where(k == h, 0, 1)
            slot = here + OTHER * other
            own.append((src, there + OTHER * (1 - other)))
            pltpu.make_async_copy(src, buf.at[slot], recv_sem.at[slot]).start()

    barrier = pltpu.get_barrier_semaphore()
    greeted = row_peers + col_peers + [outer, partner]
    for peer in greeted:
        pl.semaphore_signal(barrier, inc=1, device_id=peer, device_id_type=MESH)

    for i, row in enumerate(ITEMS):
        table[i] = pick(row)

    nt = (((1,), (1,)), ((), ()))
    blank = jnp.zeros((RANK, RANK * 8), F32)
    first = lax.dot_general(
        vectors[0], jnp.concatenate([inverse[0], blank], axis=0), nt,
        precision=lax.Precision.HIGHEST, preferred_element_type=F32,
    )
    second = lax.dot_general(
        vectors[1], jnp.concatenate([blank, inverse[1]], axis=0), nt,
        precision=lax.Precision.HIGHEST, preferred_element_type=F32,
    )
    blank = jnp.zeros((RANK, 2 * RANK), F32)
    part[...] = lax.dot_general(
        first, jnp.concatenate([first, blank], axis=0), nt,
        precision=lax.Precision.HIGHEST, preferred_element_type=F32,
    ) + lax.dot_general(
        second, jnp.concatenate([blank, second], axis=0), nt,
        precision=lax.Precision.HIGHEST, preferred_element_type=F32,
    )
    block_core[...] = jnp.zeros_like(block_core)

    pl.semaphore_wait(barrier, len(greeted))

    own_copies = []
    for i, (src, slot) in enumerate(own):
        copy = pltpu.make_async_remote_copy(
            src_ref=src, dst_ref=buf.at[slot], send_sem=own_send.at[i], recv_sem=recv_sem.at[slot],
            device_id=partner, device_id_type=MESH,
        )
        copy.start()
        own_copies.append(copy)

    def arrived(slot):
        pltpu.make_async_copy(buf.at[slot], buf.at[slot], recv_sem.at[slot]).wait()

    def panel_at(code):
        block = 2 * ((sy * (code % 4) + z + 4) % 4) + (code // 4 + flip) % 2
        return 4 * block + code // 8

    def send_of(i, word):
        way = word % 16
        src, dst = (word // 32) % 128, (word // 4096) % 128
        axis, turn = way // 2, 1 - 2 * (way % 2)
        dx = jnp.where(axis == 0, sx * turn, 0)
        dy = jnp.where(axis == 1, sy * turn, 0)
        dz = jnp.where(axis == 2, sy * turn, 0)
        dk = jnp.where(axis == 3, 1, 0)
        target = device((x + dx + 4) % 4, (y + dy + 4) % 4, (z + dz + 4) % 4, (k + dk) % 2)
        return src, pltpu.make_async_remote_copy(
            src_ref=buf.at[src], dst_ref=buf.at[dst], send_sem=send_sem.at[i],
            recv_sem=recv_sem.at[dst], device_id=target, device_id_type=MESH,
        )

    def pass_on(i, word):
        src, copy = send_of(i, word)

        @pl.when((word // 16) % 2 == 1)
        def _():
            arrived(src)

        @pl.when(word % 16 < 7)
        def _():
            copy.start()

    def moves(i, _):
        pass_on(i, table[i])
        return 0

    def prepare(block):
        codes = pick(BLOCKS[block])
        for a in range(4):
            place = 4 * block + a
            arrived(OTHER + place)
            panel = panel_at((codes // (1 << (5 * a))) % 32)
            high, low = split(buf[jnp.where(diagonal == 1, place, COL_SLOT + place)])
            wide[pl.ds(a * RANK, RANK)] = high
            wide[pl.ds(256 + a * RANK, RANK)] = high
            wide[pl.ds(512 + a * RANK, RANK)] = low
            slot = slots[panel]
            pair = known[(slot // 2) % 2 * 8 + slot // 4]
            lane = lax.broadcasted_iota(I32, (RANK, 2 * RANK), 1) // RANK
            same = jnp.where(slot % 2 == a % 2, F32(1), F32(0))
            moved = pair * same + pltpu.roll(pair, RANK, axis=1) * (F32(1) - same)
            block_core[pl.ds(a * RANK, RANK), pl.ds((a // 2) * 128, 128)] = jnp.where(
                lane == a % 2, moved, F32(0)
            )
        high, low = split(block_core[...])
        scaled = jnp.dot(
            jnp.concatenate([high, low, high], axis=1), wide[...], preferred_element_type=F32
        )
        high, low = split(scaled)
        right[0:256] = high
        right[256:512] = high
        right[512:768] = low

    def tile_rows(j):
        h = k if j * TI < HALF else 1 - k
        return pl.ds(pl.multiple_of(h * HALF + (j * TI) % HALF, TI), TI)

    def store(j):
        return pltpu.make_async_copy(acc.at[tile_rows(j)], out.at[tile_rows(j)], out_sem.at[j])

    def tile(block, j):
        if j == 0:
            prepare(block)
        base = 4 * block + (0 if j * TI < HALF else OTHER)
        left = buf[base : base + 4, :, (j * TI) % HALF : (j * TI) % HALF + TI]
        high, low = split(left.reshape(256, TI))
        rows = tile_rows(j)
        acc[rows] = acc[rows] - lax.dot_general(
            jnp.concatenate([high, low, high], axis=0), right[...], (((0,), (0,)), ((), ())),
            preferred_element_type=F32,
        )
        if block == 7 and j > 0:
            store(j - 1).start()

    lax.fori_loop(0, MARKS[0], moves, 0)
    row_copies = []
    for i, peer in enumerate(row_peers):
        copy = pltpu.make_async_remote_copy(
            src_ref=part, dst_ref=by_row.at[7 - 1 - i], send_sem=row_send.at[i],
            recv_sem=row_recv.at[7 - 1 - i], device_id=peer, device_id_type=MESH,
        )
        copy.start()
        row_copies.append(copy)
    lax.fori_loop(MARKS[0], MARKS[1], moves, 0)
    for i in range(7):
        pltpu.make_async_copy(part, by_row.at[i], row_recv.at[i]).wait()
    summed = part[...]
    for i in range(7):
        summed = summed + by_row[i]
    total[...] = summed
    lax.fori_loop(MARKS[1], MARKS[2], moves, 0)
    mine = k * 8 + q
    keep = pltpu.make_async_copy(total, cores.at[mine], local_sem.at[5])
    keep.start()
    col_copies = []
    for i, peer in enumerate(col_peers):
        copy = pltpu.make_async_remote_copy(
            src_ref=total, dst_ref=cores.at[mine], send_sem=col_send.at[i],
            recv_sem=col_recv.at[i], device_id=peer, device_id_type=MESH,
        )
        copy.start()
        col_copies.append(copy)
    lax.fori_loop(MARKS[2], MARKS[3], moves, 0)
    keep.wait()
    for i in range(7):
        sender = k * 8 + (q + 7 - i) % 8
        pltpu.make_async_copy(total, cores.at[sender], col_recv.at[i]).wait()
    half = cores.at[pl.ds(k * 8, 8)]
    exchange = pltpu.make_async_remote_copy(
        src_ref=half, dst_ref=half, send_sem=col_send.at[7], recv_sem=col_recv.at[7],
        device_id=partner, device_id_type=MESH,
    )
    exchange.start()
    lax.fori_loop(MARKS[3], MARKS[4], moves, 0)
    exchange.wait_recv()
    settle = pltpu.make_async_copy(cores, known, local_sem.at[6])
    settle.start()
    settle.wait()
    start_acc.wait()
    tiles = ROWS // TI
    done = MARKS[4]
    end = 0
    for t, length in enumerate(SEGMENTS):
        end += length
        if end > done:
            lax.fori_loop(done, end, moves, 0)
            done = end
        if t < 8 * tiles:
            tile(t // tiles, t % tiles)
    store(tiles - 1).start()

    for copy in own_copies + row_copies + col_copies + [exchange]:
        copy.wait_send()

    def sent(i, _):
        word = table[i]

        @pl.when(word % 16 < 7)
        def _():
            send_of(i, word)[1].wait_send()

        return 0

    lax.fori_loop(0, NI, sent, 0)
    for t in range(ROWS // TI):
        store(t).wait()


def body(trailing, panel_factors, vectors_t, inverse_lower_factors, slot_of_panel):
    hbm = pl.BlockSpec(memory_space=pl.ANY)
    vmem = pl.BlockSpec(memory_space=pltpu.VMEM)
    dma = pltpu.SemaphoreType.DMA
    return pl.pallas_call(
        kernel,
        out_shape=jax.ShapeDtypeStruct((ROWS, COLS), F32),
        in_specs=[hbm, hbm, vmem, vmem, pl.BlockSpec(memory_space=pltpu.SMEM)],
        out_specs=hbm,
        scratch_shapes=[
            pltpu.VMEM((ROWS, COLS), F32),
            pltpu.VMEM((SLOTS, RANK, HALF), F32),
            pltpu.VMEM((768, COLS), BF16),
            pltpu.VMEM((768, COLS), BF16),
            pltpu.VMEM((256, 256), F32),
            pltpu.VMEM((RANK, 2 * RANK), F32),
            pltpu.VMEM((7, RANK, 2 * RANK), F32),
            pltpu.VMEM((RANK, 2 * RANK), F32),
            pltpu.VMEM((16, RANK, 2 * RANK), F32),
            pltpu.VMEM((16, RANK, 2 * RANK), F32),
            pltpu.SMEM((NI,), I32),
            dma((7,)), dma((SLOTS,)), dma((NI,)), dma((4,)), dma((7,)), dma((7,)), dma((8,)), dma((8,)),
            dma((ROWS // TI,)),
        ],
        compiler_params=pltpu.CompilerParams(
            collective_id=0, has_side_effects=True, vmem_limit_bytes=56 * 2**20
        ),
        name="update",
    )(trailing, panel_factors, vectors_t, inverse_lower_factors, slot_of_panel)


def solution(mesh):
    return jax.shard_map(
        body,
        mesh=mesh,
        in_specs=(
            P("row", "col"),
            P("col", "row"),
            P("col", None, None),
            P("col", "row", None),
            P(),
        ),
        out_specs=P("row", "col"),
        check_vma=False,
    )
```

time: 394 us -> 158 us (0.40)
  waiting for transfers between devices: 241 us -> 0 us
  Pallas kernels: 0 us -> 147 us
  matrix products: 83.2 us -> 0 us
  blocking collectives: 28.2 us -> 0 us
  between operations: 13.5 us -> 0.01 us
  local copies, waits for them, and re-layouts: 14.9 us -> 8.44 us
  starting transfers between devices: 6.17 us -> 0 us
    all_to_all x1 -> x0, waiting for transfers between devices: 156 us -> none  [body(): lax.all_to_all(tall, 'col', split_axis=1, concat_axis=0, tiled=True)]
    pallas_call x0 -> x1, Pallas kernels: none -> 147 us  [body(): pl.pallas_call(kernel, out_shape=jax.ShapeDtypeStruct((ROWS, COLS), F32),...]
    all_gather x2 -> x0, waiting for transfers between devices: 84.7 us -> none  [the longest x1 75.1 us: body(): tall = lax.all_gather(panel_factors, 'row', axis=1, tiled=True)]
    dot_general x5 -> x0, matrix products: 83.2 us -> none  [the longest x1 58.2 us: body(): lax.dot_general(scaled.reshape(width, rows_blk), column_factor, (((0,), (...]
    all_to_all x2 -> x0, blocking collectives: 28.2 us -> none  [copy_for_each(): return lax.all_to_all(copies, axis, split_axis=0, concat_axis=0, tiled=True)]
    all_to_all x2 -> x0, local copies, waits for them, and re-layouts: 9.82 us -> none  [the longest x1 9.31 us: body(): lax.all_to_all(tall, 'col', split_axis=1, concat_axis=0, tiled=True)]
    all_to_all x1 -> x0, starting transfers between devices: 6.12 us -> none  [body(): lax.all_to_all(tall, 'col', split_axis=1, concat_axis=0, tiled=True)]
    unnamed x13 -> x1, local copies, waits for them, and re-layouts: 4.19 us -> 8.44 us
  transfers between devices with their start and end apart: 3 -> 0, of which waited for: 3 -> 0; matrix products, arithmetic and copies ran while one was open for 5% -> 0% of each run, Pallas kernels for 0% -> 0%
where the time goes in v1:
time: 158 us; the launch traced here: 155 us
  Pallas kernels  147 us (93%)
  local copies, waits for them, and re-layouts  8.44 us (5%)
    pallas_call x1, Pallas kernels, body(): pl.pallas_call(kernel, out_shape=jax.ShapeDtypeStruct((ROWS, COLS), F32),...  147 us
    unnamed x1, local copies, waits for them, and re-layouts  8.44 us

profile of v1, /device:TPU:26, one launch (start us, length us, event | category | flops | bytes accessed | tf_op | source)
XLA Modules:
  0.0 155.2 jit_solution(12734521453328167814)
XLA Ops:
  0.0 146.8 %update.1 = f32[2048,1024]{1,0:T(8,128)} custom-call(f32[2048,1024]{1,0:T(8,128)} %trailing.1, f32[128,2048]{1,0:T(8,128)} %factors.1, f32[2,64,512]{2,1,0:T(8,128)} %vectors.1, f32[2,64,512]{2,1,0:T(8,128)} %inverse.1, s32[32]{0:T(128)} %slots.1), custom_call_target="tpu_custom_call" | custom-call | tf_op jit(solution)/shard_map/update/pallas_call | solution.py:479
  146.8 8.4 %copy.7 = f32[2048,1024]{1,0:T(8,128)} copy(f32[2048,1024]{1,0:T(8,128)} %update.1) | data formatting | bytes 16777216

commit v2 on v0

v2 whole, which is shorter than its diff:
```python
import jax
import jax.numpy as jnp
from jax import lax
from jax.experimental import pallas as pl
from jax.experimental.pallas import tpu as pltpu
from jax.sharding import PartitionSpec as P

MESH = pl.DeviceIdType.MESH
F32, BF16, I32 = jnp.float32, jnp.bfloat16, jnp.int32

ITEMS = (
    (9, 9, 9, 9, 9, 9, 9, 9),
    (8243, 16592, 33040, 29042, 17265, 438800, 422256, 16883),
    (127088, 10, 4274, 77939, 4947, 29233, 107249, 397909),
    (450641, 24691, 10, 393237, 10, 90659, 37219, 10),
    (262213, 11, 77875, 10, 20529, 10, 10, 421904),
    (10, 95059, 11, 28768, 111458, 57890, 25314, 53825),
    (94227, 102642, 69648, 74387, 11, 61555, 11, 11),
    (11, 397541, 32771, 11, 21314, 11, 98322, 16433),
    (262244, 209126, 49776, 12643, 408626, 53762, 16529, 401445),
    (16386, 264213, 160358, 401493, 70353, 273779, 401541, 151590),
    (12528, 8290, 4259, 139334, 213702, 393364, 188550, 110707),
    (463073, 77843, 238422, 16432, 86051, 159878, 412913, 123089),
    (266468, 107120, 306227, 135206, 263152, 442672, 33042, 69874),
    (155878, 201318, 20738, 268308, 54242, 82209, 86275, 37058),
    (359442, 28866, 393813, 119218, 95203, 24867, 164102, 147686),
    (65600, 37059, 188998, 24995, 259046, 168230, 410068, 159942),
    (8226, 12, 12, 430501, 303600, 430960, 147910, 400467),
    (37011, 409876, 49970, 180646, 209382, 21345, 102514, 310514),
    (147590, 188678, 148262, 90864, 41793, 66402, 12, 429284),
    (269776, 45200, 77970, 398053, 12, 140134, 66417, 12),
    (8400, 422020, 53379, 148198, 396307, 12, 123747, 16530),
    (270532, 225414, 233606, 12, 333908, 282003, 217958, 135302),
    (266437, 205462, 440337, 119424, 416850, 110609, 123442, 418576),
    (159942, 13, 13, 32866, 139382, 404626, 8739, 41729),
    (277586, 419889, 4208, 272436, 13, 388403, 201254, 33538),
    (12, 276517, 65635, 13, 264212, 429348, 322834, 221958),
    (54000, 4144, 139366, 396307, 264197, 13, 453891, 406197),
    (459489, 45091, 2103, 69779, 344624, 21171, 13, 225958),
    (221926, 405540, 8272, 254086, 180774, 164518, 37297, 13),
    (446641, 135206, 24642, 434485, 53457, 426160, 49570, 268852),
    (118946, 412401, 143430, 151846, 155846, 123041, 168358, 294098),
    (28835, 309989, 272468, 49330, 9059, 106658, 94305, 176854),
    (151718, 53426, 57346, 221350, 119314, 135334, 29411, 217366),
    (339504, 442532, 113809, 415825, 20995, 69729, 416816, 99059),
    (286002, 168102, 168150, 114688, 197126, 459600, 76836, 185062),
    (13, 280917, 277872, 62418, 420978, 119618, 82323, 426928),
    (41584, 49234, 2167, 172998, 285012, 29507, 151942, 103330),
    (352868, 426052, 7, 114931, 272709, 189254, 197142, 164774),
    (295525, 139334, 7, 438501, 65553, 238550, 411696, 264212),
    (205414, 302288, 7, 250086, 306451, 326768, 268324, 115506),
    (7, 2135, 7, 184726, 282928, 76900, 41010, 230182),
    (7, 32768, 7, 338644, 168230, 40962, 24611, 77922),
    (7, 45890, 7, 273584, 288917, 82290, 139302, 269328),
    (7, 127859, 7, 123219, 276532, 425236, 420944, 115603),
    (7, 416019, 7, 176454, 276517, 221542, 68677, 234374),
    (7, 246630, 7, 160374, 49746, 197206, 416949, 403633),
    (7, 284789, 7, 346612, 188998, 86114, 230166, 86994),
    (7, 306320, 7, 428593, 289428, 298515, 37218, 140230),
    (7, 7, 7, 2231, 285317, 433668, 238422, 409680),
    (7, 7, 7, 53456, 40962, 2071, 2071, 241734),
    (7, 7, 7, 196806, 2423, 254038, 135254, 343314),
    (7, 7, 7, 293969, 294131, 225718, 58290, 205334),
    (7, 7, 7, 322611, 45059, 147510, 250790, 285875),
    (7, 7, 7, 432241, 3031, 2103, 289937, 280628),
    (7, 7, 7, 297060, 319568, 276980, 280661, 408017),
    (7, 7, 7, 74370, 143430, 272869, 90449, 338372),
    (7, 7, 7, 350484, 343347, 434720, 160070, 114689),
    (7, 7, 7, 363792, 346292, 403537, 78739, 123059),
    (7, 7, 7, 7, 346277, 325701, 205702, 250022),
    (7, 7, 7, 7, 286864, 433621, 2167, 2135),
    (7, 7, 7, 7, 147590, 281776, 457940, 2167),
    (7, 7, 7, 7, 299184, 294049, 2551, 7),
    (7, 7, 7, 7, 151718, 98307, 7, 7),
    (7, 7, 7, 7, 2167, 301365, 7, 7),
    (7, 7, 7, 7, 7, 288981, 7, 7),
    (7, 7, 7, 7, 7, 314707, 7, 7),
    (7, 7, 7, 7, 7, 127250, 7, 7),
    (7, 7, 7, 7, 7, 250118, 7, 7),
    (7, 7, 7, 7, 7, 41201, 7, 7),
    (7, 7, 7, 7, 7, 155878, 7, 7),
    (7, 7, 7, 7, 7, 152502, 7, 7),
    (7, 7, 7, 7, 7, 57859, 7, 7),
    (7, 7, 7, 7, 7, 49665, 7, 7),
    (7, 7, 7, 7, 7, 297109, 7, 7),
    (7, 7, 7, 7, 7, 314866, 7, 7),
    (7, 7, 7, 7, 7, 2167, 7, 7),
    (246710, 57779, 20720, 86482, 176566, 395600, 7, 37443),
    (188982, 180646, 32994, 418245, 7, 358724, 7, 2199),
    (7, 148438, 209126, 164294, 7, 305477, 7, 7),
    (7, 355568, 334197, 2199, 7, 213654, 7, 7),
    (7, 343265, 119314, 40963, 7, 298192, 7, 7),
    (7, 445669, 250374, 7, 7, 7, 7, 7),
    (289842, 160694, 90371, 306289, 82193, 321717, 7, 421013),
    (326803, 119346, 76820, 310480, 164102, 7, 7, 7),
    (364048, 107043, 400389, 371905, 2519, 7, 7, 7),
    (425477, 250406, 242550, 313556, 7, 7, 7, 7),
    (7, 7, 7, 90114, 7, 7, 7, 7),
    (7, 7, 7, 317972, 7, 7, 7, 7),
    (49456, 156182, 280725, 168214, 159990, 7, 180406, 65937),
    (454945, 7, 7, 2295, 7, 7, 32048, 180614),
    (164134, 7, 7, 7, 7, 7, 395408, 436563),
    (37138, 7, 7, 7, 7, 7, 292996, 156086),
    (282884, 7, 7, 7, 7, 7, 213654, 2263),
    (278789, 7, 7, 7, 7, 7, 407728, 7),
    (168198, 7, 7, 7, 7, 7, 309412, 7),
    (7, 7, 7, 7, 7, 7, 297125, 7),
    (172374, 293013, 184758, 7, 301652, 184534, 69842, 188758),
    (7, 301237, 155958, 7, 313556, 48148, 61635, 411889),
    (7, 57440, 2647, 7, 313541, 61841, 155846, 383205),
    (7, 115280, 201270, 7, 342261, 180614, 408145, 2711),
    (7, 193094, 436401, 7, 322770, 2775, 318020, 7),
    (7, 322641, 24976, 7, 7, 2295, 107186, 7),
    (7, 420933, 180614, 7, 7, 7, 242342, 7),
    (7, 2679, 103154, 7, 7, 7, 254934, 7),
    (7, 152278, 58083, 7, 7, 7, 2359, 7),
    (7, 2359, 226022, 7, 7, 7, 317653, 7),
    (7, 415953, 424593, 7, 7, 7, 127219, 7),
    (7, 2295, 294288, 7, 7, 7, 172262, 7),
    (7, 7, 306561, 7, 7, 7, 98403, 7),
    (7, 7, 421253, 7, 7, 7, 416017, 7),
    (7, 7, 246678, 7, 7, 7, 193526, 7),
    (7, 7, 310608, 7, 7, 7, 184630, 7),
    (7, 7, 127346, 7, 7, 7, 2295, 7),
    (7, 7, 172390, 7, 7, 7, 7, 7),
    (7, 7, 69666, 7, 7, 7, 7, 7),
    (7, 7, 346324, 7, 7, 7, 7, 7),
    (7, 7, 301253, 7, 7, 7, 7, 7),
    (7, 7, 2295, 7, 7, 7, 7, 7),
    (314706, 233942, 46035, 62355, 2327, 334101, 343057, 2839),
    (396530, 2519, 254918, 242566, 323920, 346773, 7, 94210),
    (277731, 2551, 355568, 201654, 233798, 172502, 7, 7),
    (331184, 164150, 99250, 403891, 7, 258678, 7, 7),
    (176502, 7, 197542, 326324, 7, 115025, 7, 7),
    (295316, 7, 2327, 326960, 7, 414020, 7, 7),
    (299397, 7, 7, 2359, 7, 176454, 7, 7),
    (180614, 7, 7, 7, 7, 7, 7, 7),
    (328116, 7, 111314, 7, 330036, 403824, 2391, 7),
    (324005, 7, 193222, 7, 338213, 334180, 7, 7),
    (184742, 7, 338229, 7, 172854, 7, 7, 7),
    (7, 7, 432593, 7, 7, 7, 7, 7),
    (7, 7, 350660, 7, 7, 7, 7, 7),
    (7, 7, 321989, 7, 7, 7, 7, 7),
    (335218, 254294, 102560, 7, 2807, 7, 330100, 317748),
    (289907, 7, 7, 7, 7, 7, 338277, 74033),
    (355824, 7, 7, 7, 7, 7, 350612, 168230),
    (7, 7, 7, 7, 7, 7, 354693, 86385),
    (7, 7, 7, 7, 7, 7, 449876, 78179),
    (7, 7, 7, 7, 7, 7, 7, 409957),
    (7, 7, 7, 7, 7, 7, 7, 172390),
    (7, 7, 7, 7, 7, 7, 7, 2327),
    (7, 7, 7, 7, 7, 7, 7, 2423),
    (349172, 103232, 127315, 2391, 316176, 62354, 375220, 330132),
    (308197, 335024, 176454, 193046, 78595, 2455, 7, 7),
    (254950, 2711, 2743, 189238, 226054, 242566, 7, 7),
    (7, 2423, 2391, 2423, 94242, 7, 7, 7),
    (7, 172406, 330961, 7, 2839, 7, 7, 7),
    (7, 2455, 355441, 7, 2999, 7, 7, 7),
    (7, 7, 330132, 7, 184694, 7, 7, 7),
    (7, 7, 7, 7, 349072, 7, 7, 7),
    (7, 7, 7, 7, 99201, 7, 7, 7),
    (7, 7, 7, 7, 246662, 7, 7, 7),
    (311796, 184726, 98803, 2647, 350708, 201206, 367729, 238038),
    (315877, 57346, 221670, 2455, 362981, 2487, 209526, 342644),
    (192998, 408241, 351536, 2903, 2455, 85076, 2519, 2487),
    (318867, 7, 7, 127984, 82323, 2519, 90115, 358900),
    (197142, 7, 7, 259046, 201094, 74546, 387796, 7),
    (64692, 7, 7, 343185, 7, 246566, 371397, 7),
    (310547, 7, 7, 424401, 7, 363125, 258550, 7),
    (7, 334261, 2487, 82643, 7, 7, 7, 7),
    (7, 89109, 7, 217798, 7, 7, 7, 7),
    (7, 7, 7, 111088, 7, 7, 7, 7),
    (7, 7, 7, 205286, 7, 7, 7, 7),
    (201174, 259062, 400468, 7, 425106, 7, 7, 371220),
    (7, 7, 371889, 7, 365168, 7, 7, 193078),
    (7, 7, 7, 7, 103009, 7, 7, 258678),
    (7, 7, 7, 7, 193126, 7, 7, 7),
    (7, 7, 7, 7, 408755, 7, 7, 7),
    (7, 7, 7, 7, 358836, 7, 7, 7),
    (7, 7, 7, 7, 371109, 7, 7, 7),
    (234326, 197110, 205270, 7, 115153, 209910, 2583, 7),
    (7, 359536, 2551, 7, 205254, 90866, 383541, 7),
    (7, 7, 7, 7, 377520, 217830, 246358, 7),
    (7, 7, 7, 7, 217766, 7, 7, 7),
    (209494, 363285, 2583, 111154, 2583, 399920, 234294, 399952),
    (90179, 2583, 2615, 209446, 2615, 371236, 7, 375365),
    (339154, 358965, 354932, 213590, 221846, 2583, 7, 209910),
    (361109, 7, 359013, 127827, 375476, 2647, 7, 7),
    (213638, 7, 213654, 226118, 379557, 234262, 7, 7),
    (217782, 7, 217782, 2679, 2679, 7, 7, 7),
    (7, 7, 7, 367856, 7, 7, 7, 7),
    (7, 7, 7, 2711, 7, 7, 7, 7),
    (7, 7, 7, 234262, 7, 7, 7, 7),
    (7, 7, 7, 246454, 7, 7, 7, 7),
    (7, 99218, 7, 7, 7, 367856, 428657, 254806),
    (7, 217990, 7, 7, 7, 376033, 391780, 213654),
    (7, 7, 7, 7, 7, 7, 221910, 7),
    (7, 242454, 379604, 7, 123633, 230102, 2711, 2743),
    (7, 375858, 375573, 7, 230118, 2743, 7, 7),
    (7, 7, 7, 7, 2775, 7, 7, 7),
    (226006, 2647, 230166, 230262, 7, 2807, 7, 7),
    (7, 221878, 7, 7, 7, 375573, 7, 7),
    (7, 7, 7, 7, 7, 121908, 7, 7),
    (7, 379701, 383733, 2839, 387892, 368050, 2743, 246646),
    (7, 7, 387892, 7, 383781, 7, 2807, 380016),
    (7, 7, 387877, 7, 7, 7, 7, 380001),
    (7, 7, 7, 7, 7, 7, 7, 2775),
    (106595, 238326, 2903, 2807, 2903, 7, 391957, 2807),
    (7, 2775, 7, 7, 2935, 7, 7, 126005),
    (7, 230198, 259062, 7, 7, 2871, 7, 2871),
    (7, 7, 2935, 7, 7, 379733, 7, 7),
    (86082, 7, 7, 383796, 7, 7, 7, 7),
    (344132, 387957, 2967, 2935, 2967, 7, 2871, 2903),
    (7, 2903, 7, 7, 250806, 7, 2903, 383892),
    (7, 2967, 7, 7, 7, 7, 2935, 392069),
    (7, 7, 7, 7, 7, 7, 7, 2935),
    (7, 2999, 392465, 2967, 254934, 2935, 7, 7),
    (7, 7, 7, 7, 7, 387989, 7, 7),
    (361236, 7, 7, 7, 7, 7, 7, 7),
    (365317, 7, 7, 7, 7, 7, 7, 7),
    (230150, 7, 7, 7, 7, 7, 7, 7),
    (368741, 7, 7, 7, 7, 7, 7, 2999),
    (94306, 7, 7, 7, 7, 7, 7, 7),
    (103218, 7, 7, 7, 7, 7, 7, 7),
    (365348, 7, 7, 7, 7, 7, 7, 7),
    (381733, 7, 7, 7, 7, 7, 7, 7),
    (238374, 7, 7, 7, 7, 7, 7, 7),
    (242550, 7, 7, 7, 7, 7, 7, 7),
    (250774, 7, 7, 7, 7, 7, 7, 7),
    (7, 3031, 2999, 2999, 7, 392117, 2967, 3031),
    (7, 7, 7, 7, 7, 3031, 2999, 7),
    (7, 7, 3031, 7, 3063, 7, 7, 7),
    (7, 7, 392180, 3031, 7, 3063, 3031, 3063),
    (7, 7, 392165, 7, 7, 7, 7, 7),
    (259030, 3063, 7, 3063, 7, 7, 3063, 7),
)
SEGMENTS = (76, 6, 6, 8, 22, 8, 6, 9, 10, 7, 4, 7, 4, 10, 3, 3, 3, 4, 2, 2, 1, 4, 2, 3, 8, 2, 1, 2, 1, 0, 0, 0, 0)
BLOCKS = (
    (803072, 303441, 370514, 106843, 370332, 706909, 730494, 766111),
    (370316, 165248, 48455, 664644, 866378, 208001, 1024039, 104970),
    (331811, 989298, 847266, 391553, 902366, 29137, 488930, 929218),
    (204226, 514285, 1033608, 575973, 702241, 272143, 628131, 256301),
    (576700, 872107, 117911, 244557, 769136, 892077, 943692, 965893),
    (847454, 789006, 750608, 17299, 1021511, 686147, 217760, 787073),
    (874230, 976639, 465084, 975573, 397949, 420662, 758104, 579294),
    (982509, 889500, 817844, 826111, 794646, 1039891, 574299, 838267),
)
OWN = ((0, 6, 8, 3, 26, 17, 23, 15), (1, 3, 5, 11, 27, 16, 11, 18), (2, 0, 0, 20, 1, 3, 3, 3), (3, 26, 1, 0, 0, 0, 0, 0))
PARTNERS = ((0, 3, 8, 6, 26, 15, 23, 17), (1, 11, 5, 3, 27, 18, 11, 16), (2, 20, 0, 0, 1, 3, 3, 3), (3, 0, 1, 26, 0, 0, 0, 0))
TRANSIT = 18
TI = 512

ROWS, COLS, RANK, HALF = 2048, 1024, 64, 1024
OTHER, COL_SLOT, TRANSIT_SLOT = 32, 64, 96
SLOTS = TRANSIT_SLOT + TRANSIT
NI = len(ITEMS)


def split(x):
    high = x.astype(BF16)
    return high, (x - high.astype(F32)).astype(BF16)


def kernel(
    trailing, factors, vectors, inverse, slots, acc,
    buf, right, wide, block_core, part, by_row, total, cores, known, table,
    local_sem, recv_sem, send_sem, own_send, row_send, row_recv, col_send, col_recv,
):
    r, c = lax.axis_index("row"), lax.axis_index("col")
    z, x, y, k = r // 2, (r % 2) * 2 + (c // 2) % 2, c // 4, c % 2
    flip = x // 2
    sx, sy = 1 - 2 * flip, 1 - 2 * k
    xc = x + flip * (3 - 2 * x)
    delta = (sy * (y - z) + 4) % 4
    kind = xc * 4 + delta
    diagonal = jnp.where(kind == 0, 1, 0)
    q = c // 2

    def device(x, y, z, k):
        return (z * 2 + x // 2, y * 4 + (x % 2) * 2 + k)

    partner = (r, q * 2 + 1 - k)
    row_peers = [((r + i) % 8, c) for i in range(1, 8)]
    col_peers = [(r, (c + 2 * i) % 16) for i in range(1, 8)]
    outer = device(3 - x, y, z, k)

    start_acc = pltpu.make_async_copy(trailing, acc, local_sem.at[4])
    start_acc.start()
    bits = [kind % 2 == 1, (kind // 2) % 2 == 1, kind // 4 == 1]

    def pick(row):
        pairs = [jnp.where(bits[0], I32(row[2 * a + 1]), I32(row[2 * a])) for a in range(4)]
        pairs = [jnp.where(bits[1], pairs[2 * a + 1], pairs[2 * a]) for a in range(2)]
        return jnp.where(bits[2], pairs[1], pairs[0])

    own = []
    for j in range(2):
        here = jnp.where(k == 0, pick(OWN[j]), pick(OWN[2 + j]))
        there = jnp.where(k == 0, pick(PARTNERS[j]), pick(PARTNERS[2 + j]))
        for h in range(2):
            src = factors.at[pl.ds(j * RANK, RANK), pl.ds(h * HALF, HALF)]
            other = jnp.where(k == h, 0, 1)
            slot = here + OTHER * other
            own.append((src, there + OTHER * (1 - other)))
            pltpu.make_async_copy(src, buf.at[slot], recv_sem.at[slot]).start()

    barrier = pltpu.get_barrier_semaphore()
    greeted = row_peers + col_peers + [outer, partner]
    for peer in greeted:
        pl.semaphore_signal(barrier, inc=1, device_id=peer, device_id_type=MESH)

    for i, row in enumerate(ITEMS):
        table[i] = pick(row)

    nt = (((1,), (1,)), ((), ()))
    blank = jnp.zeros((RANK, RANK * 8), F32)
    first = lax.dot_general(
        vectors[0], jnp.concatenate([inverse[0], blank], axis=0), nt,
        precision=lax.Precision.HIGHEST, preferred_element_type=F32,
    )
    second = lax.dot_general(
        vectors[1], jnp.concatenate([blank, inverse[1]], axis=0), nt,
        precision=lax.Precision.HIGHEST, preferred_element_type=F32,
    )
    blank = jnp.zeros((RANK, 2 * RANK), F32)
    part[...] = lax.dot_general(
        first, jnp.concatenate([first, blank], axis=0), nt,
        precision=lax.Precision.HIGHEST, preferred_element_type=F32,
    ) + lax.dot_general(
        second, jnp.concatenate([blank, second], axis=0), nt,
        precision=lax.Precision.HIGHEST, preferred_element_type=F32,
    )
    block_core[...] = jnp.zeros_like(block_core)

    pl.semaphore_wait(barrier, len(greeted))

    own_copies = []
    for i, (src, slot) in enumerate(own):
        copy = pltpu.make_async_remote_copy(
            src_ref=src, dst_ref=buf.at[slot], send_sem=own_send.at[i], recv_sem=recv_sem.at[slot],
            device_id=partner, device_id_type=MESH,
        )
        copy.start()
        own_copies.append(copy)

    def arrived(slot):
        pltpu.make_async_copy(buf.at[slot], buf.at[slot], recv_sem.at[slot]).wait()

    def panel_at(code):
        block = 2 * ((sy * (code % 4) + z + 4) % 4) + (code // 4 + flip) % 2
        return 4 * block + code // 8

    def send_of(i, word):
        way = word % 16
        src, dst = (word // 32) % 128, (word // 4096) % 128
        axis, turn = way // 2, 1 - 2 * (way % 2)
        dx = jnp.where(axis == 0, sx * turn, 0)
        dy = jnp.where(axis == 1, sy * turn, 0)
        dz = jnp.where(axis == 2, sy * turn, 0)
        dk = jnp.where(axis == 3, 1, 0)
        target = device((x + dx + 4) % 4, (y + dy + 4) % 4, (z + dz + 4) % 4, (k + dk) % 2)
        return src, pltpu.make_async_remote_copy(
            src_ref=buf.at[src], dst_ref=buf.at[dst], send_sem=send_sem.at[i],
            recv_sem=recv_sem.at[dst], device_id=target, device_id_type=MESH,
        )

    def pass_on(i, word):
        src, copy = send_of(i, word)

        @pl.when((word // 16) % 2 == 1)
        def _():
            arrived(src)

        @pl.when(word % 16 < 7)
        def _():
            copy.start()

    def moves(i, _):
        pass_on(i, table[i])
        return 0

    def sent(i, _):
        @pl.when(table[i] % 16 < 7)
        def _():
            pltpu.make_async_copy(buf.at[0], buf.at[0], send_sem.at[i]).wait()

        return 0

    def prepare(block):
        codes = pick(BLOCKS[block])
        for a in range(4):
            place = 4 * block + a
            arrived(OTHER + place)
            panel = panel_at((codes // (1 << (5 * a))) % 32)
            high, low = split(buf[jnp.where(diagonal == 1, place, COL_SLOT + place)])
            wide[pl.ds(a * RANK, RANK)] = high
            wide[pl.ds(256 + a * RANK, RANK)] = high
            wide[pl.ds(512 + a * RANK, RANK)] = low
            slot = slots[panel]
            pair = known[(slot // 2) % 2 * 8 + slot // 4]
            lane = lax.broadcasted_iota(I32, (RANK, 2 * RANK), 1) // RANK
            same = jnp.where(slot % 2 == a % 2, F32(1), F32(0))
            moved = pair * same + pltpu.roll(pair, RANK, axis=1) * (F32(1) - same)
            block_core[pl.ds(a * RANK, RANK), pl.ds((a // 2) * 128, 128)] = jnp.where(
                lane == a % 2, moved, F32(0)
            )
        high, low = split(block_core[...])
        scaled = jnp.dot(
            jnp.concatenate([high, low, high], axis=1), wide[...], preferred_element_type=F32
        )
        high, low = split(scaled)
        right[0:256] = high
        right[256:512] = high
        right[512:768] = low

    def tile_rows(j):
        h = k if j * TI < HALF else 1 - k
        return pl.ds(pl.multiple_of(h * HALF + (j * TI) % HALF, TI), TI)

    def tile(block, j):
        if j == 0:
            prepare(block)
        base = 4 * block + (0 if j * TI < HALF else OTHER)
        left = buf[base : base + 4, :, (j * TI) % HALF : (j * TI) % HALF + TI]
        high, low = split(left.reshape(256, TI))
        rows = tile_rows(j)
        acc[rows] = acc[rows] - lax.dot_general(
            jnp.concatenate([high, low, high], axis=0), right[...], (((0,), (0,)), ((), ())),
            preferred_element_type=F32,
        )

    mine = k * 8 + q
    row_copies = [
        pltpu.make_async_remote_copy(
            src_ref=part, dst_ref=by_row.at[6 - i], send_sem=row_send.at[i],
            recv_sem=row_recv.at[6 - i], device_id=peer, device_id_type=MESH,
        )
        for i, peer in enumerate(row_peers)
    ]
    keep = pltpu.make_async_copy(total, cores.at[mine], local_sem.at[5])
    col_copies = [
        pltpu.make_async_remote_copy(
            src_ref=total, dst_ref=cores.at[mine], send_sem=col_send.at[i],
            recv_sem=col_recv.at[i], device_id=peer, device_id_type=MESH,
        )
        for i, peer in enumerate(col_peers)
    ]
    half = cores.at[pl.ds(k * 8, 8)]
    exchange = pltpu.make_async_remote_copy(
        src_ref=half, dst_ref=half, send_sem=col_send.at[7], recv_sem=col_recv.at[7],
        device_id=partner, device_id_type=MESH,
    )
    settle = pltpu.make_async_copy(cores, known, local_sem.at[6])

    def give_share():
        for copy in row_copies:
            copy.start()

    def add_shares():
        for i in range(7):
            pltpu.make_async_copy(part, by_row.at[i], row_recv.at[i]).wait()
        summed = part[...]
        for i in range(7):
            summed = summed + by_row[i]
        total[...] = summed

    def give_total():
        keep.start()
        for copy in col_copies:
            copy.start()

    def give_half():
        keep.wait()
        for i in range(7):
            sender = k * 8 + (q + 7 - i) % 8
            pltpu.make_async_copy(total, cores.at[sender], col_recv.at[i]).wait()
        exchange.start()

    def take_half():
        exchange.wait_recv()
        settle.start()
        settle.wait()
        start_acc.wait()

    def opening(i, _):
        word = table[i]

        @pl.when(word % 16 < 8)
        def _():
            pass_on(i, word)

        for phase, action in enumerate((give_share, add_shares, give_total, give_half, take_half)):
            pl.when(word % 16 == 9 + phase)(action)
        return 0

    lax.fori_loop(0, SEGMENTS[0], opening, 0)
    tiles = ROWS // TI
    done = SEGMENTS[0]
    end = checked = 0
    for t, length in enumerate(SEGMENTS):
        end += length
        if end > done:
            lax.fori_loop(done, end, moves, 0)
            done = end
        if t in (4 * tiles, 7 * tiles):
            early = sum(SEGMENTS[: t - tiles])
            lax.fori_loop(checked, early, sent, 0)
            checked = early
        if t < 8 * tiles:
            tile(t // tiles, t % tiles)

    for copy in own_copies + row_copies + col_copies + [exchange]:
        copy.wait_send()

    lax.fori_loop(checked, NI, sent, 0)


def body(trailing, panel_factors, vectors_t, inverse_lower_factors, slot_of_panel):
    hbm = pl.BlockSpec(memory_space=pl.ANY)
    vmem = pl.BlockSpec(memory_space=pltpu.VMEM)
    dma = pltpu.SemaphoreType.DMA
    return pl.pallas_call(
        kernel,
        out_shape=pltpu.VMEM((ROWS, COLS), F32),
        in_specs=[hbm, hbm, vmem, vmem, pl.BlockSpec(memory_space=pltpu.SMEM)],
        out_specs=vmem,
        scratch_shapes=[
            pltpu.VMEM((SLOTS, RANK, HALF), F32),
            pltpu.VMEM((768, COLS), BF16),
            pltpu.VMEM((768, COLS), BF16),
            pltpu.VMEM((256, 256), F32),
            pltpu.VMEM((RANK, 2 * RANK), F32),
            pltpu.VMEM((7, RANK, 2 * RANK), F32),
            pltpu.VMEM((RANK, 2 * RANK), F32),
            pltpu.VMEM((16, RANK, 2 * RANK), F32),
            pltpu.VMEM((16, RANK, 2 * RANK), F32),
            pltpu.SMEM((NI,), I32),
            dma((7,)), dma((SLOTS,)), dma((NI,)), dma((4,)), dma((7,)), dma((7,)), dma((8,)), dma((8,)),
        ],
        compiler_params=pltpu.CompilerParams(
            collective_id=0, has_side_effects=True, vmem_limit_bytes=55 * 2**20
        ),
        name="update",
    )(trailing, panel_factors, vectors_t, inverse_lower_factors, slot_of_panel)


def solution(mesh):
    return jax.shard_map(
        body,
        mesh=mesh,
        in_specs=(
            P("row", "col"),
            P("col", "row"),
            P("col", None, None),
            P("col", "row", None),
            P(),
        ),
        out_specs=P("row", "col"),
        check_vma=False,
    )
```

time: 394 us -> 134 us (0.34)
  the two profiles are of different devices: /device:TPU:26 before, /device:TPU:66 now
where the time goes in v2:
time: 134 us
  Pallas kernels  131 us (98%)
  local copies, waits for them, and re-layouts  3.4 us (3%)
    pallas_call x1, Pallas kernels, body(): pl.pallas_call(kernel, out_shape=pltpu.VMEM((ROWS, COLS), F32), in_specs=...  131 us
    unnamed x1, local copies, waits for them, and re-layouts  3.4 us

profile of v2, /device:TPU:66, one launch (start us, length us, event | category | flops | bytes accessed | tf_op | source)
XLA Modules:
  0.0 134.2 jit_solution(9885874576379836634)
XLA Ops:
  0.0 130.8 %update.1 = f32[2048,1024]{1,0:T(8,128)S(1)} custom-call(f32[2048,1024]{1,0:T(8,128)} %trailing.1, f32[128,2048]{1,0:T(8,128)} %factors.1, f32[2,64,512]{2,1,0:T(8,128)} %vectors.1, f32[2,64,512]{2,1,0:T(8,128)} %inverse.1, s32[32]{0:T(128)} %slots.1), custom_call_target="tpu_custom_call" | custom-call | tf_op jit(solution)/shard_map/update/pallas_call | solution.py:522
  130.8 3.4 %copy.7 = f32[2048,1024]{1,0:T(8,128)} copy(f32[2048,1024]{1,0:T(8,128)S(1)} %update.1) | data formatting | bytes 16777216

commit v3 on v2

v3 whole, which is shorter than its diff:
```python
import jax
import jax.numpy as jnp
from jax import lax
from jax.experimental import pallas as pl
from jax.experimental.pallas import tpu as pltpu
from jax.sharding import PartitionSpec as P

MESH = pl.DeviceIdType.MESH
F32, BF16, I32 = jnp.float32, jnp.bfloat16, jnp.int32

ITEMS = (
    (9, 9, 9, 9, 9, 9, 9, 9),
    (8240, 24754, 16, 24656, 16497, 430096, 20561, 61489),
    (458769, 397476, 33106, 426049, 24674, 45426, 41267, 393397),
    (36866, 10, 10, 36914, 413748, 78179, 10, 10),
    (262181, 57392, 4144, 10, 262288, 10, 102609, 430192),
    (10, 74227, 20482, 86051, 10, 107057, 90179, 65634),
    (3, 11, 11, 394069, 29107, 11, 11, 49251),
    (266325, 12304, 58098, 11, 413733, 401956, 45250, 397813),
    (11, 8496, 28882, 45555, 11, 286003, 49521, 11),
    (64, 413988, 393412, 418277, 20513, 417060, 41314, 49362),
    (265267, 131366, 139462, 139750, 404498, 434512, 151910, 16579),
    (82224, 264213, 65570, 24850, 307824, 422096, 99091, 241862),
    (467233, 110752, 37042, 429331, 156262, 82241, 65554, 281776),
    (348453, 107346, 65699, 164102, 266320, 28866, 28675, 429220),
    (160038, 107331, 151718, 49218, 139334, 90435, 131078, 392498),
    (446609, 181062, 430769, 16, 317460, 139462, 265488, 418032),
    (16514, 268341, 144038, 16387, 321541, 168262, 397717, 82145),
    (24707, 396304, 57664, 405509, 119313, 8193, 164230, 164070),
    (147590, 12, 2071, 167942, 246278, 53714, 12, 12),
    (278032, 414353, 12, 393396, 12, 184774, 90353, 426352),
    (367634, 205446, 70003, 155814, 408626, 277680, 8418, 209254),
    (365140, 277173, 205158, 91056, 404563, 273569, 159974, 12449),
    (188998, 82402, 41778, 86850, 73762, 45409, 86066, 36898),
    (12, 13, 95011, 12, 2231, 438992, 86051, 412723),
    (291028, 438420, 234278, 415761, 278544, 70339, 135206, 13),
    (155846, 155782, 13, 272388, 94210, 201414, 13, 272533),
    (273587, 168470, 86752, 410069, 81923, 12, 20627, 86113),
    (12466, 73810, 398164, 184774, 131078, 273488, 143494, 61459),
    (16547, 90179, 441651, 322356, 264564, 281665, 397748, 139270),
    (151718, 421956, 185158, 13, 280933, 27716, 237990, 2487),
    (302672, 192582, 310290, 115347, 363699, 420933, 277712, 53585),
    (277714, 28675, 2103, 180870, 13, 110706, 314561, 168262),
    (13, 453812, 11537, 280820, 287120, 20579, 2071, 379984),
    (462961, 119344, 437507, 147670, 176518, 147558, 49618, 416835),
    (266276, 430628, 201110, 106736, 33489, 384339, 16835, 76869),
    (226134, 420657, 78480, 159974, 221894, 437573, 188870, 421077),
    (295316, 301861, 115330, 273584, 37074, 13, 286035, 20643),
    (285810, 201254, 189062, 2103, 209094, 412113, 109716, 111314),
    (172422, 12290, 284789, 65650, 66194, 268741, 408709, 180934),
    (7, 41123, 297044, 176230, 17027, 107283, 127858, 2071),
    (7, 404530, 147606, 432209, 152198, 209670, 172902, 160278),
    (7, 284757, 221910, 61970, 268340, 131158, 94898, 82579),
    (7, 367824, 155734, 258566, 264229, 429300, 53923, 225926),
    (7, 426740, 408016, 289044, 3063, 114739, 217766, 326930),
    (7, 442484, 317892, 58274, 45617, 392304, 2103, 152406),
    (7, 172774, 24579, 286000, 201254, 314465, 2167, 272436),
    (7, 147558, 176726, 123571, 2135, 31844, 28961, 405589),
    (7, 36898, 399664, 172710, 276628, 32771, 37154, 155718),
    (7, 401412, 330021, 99139, 268421, 280725, 193014, 425075),
    (7, 297941, 246678, 143510, 290067, 450800, 2199, 305940),
    (7, 53619, 338325, 196918, 2167, 57571, 78019, 359317),
    (7, 143718, 45170, 2231, 7, 196838, 445456, 284756),
    (7, 428305, 217190, 250294, 7, 396338, 35845, 2167),
    (7, 407665, 415889, 292980, 7, 447344, 74354, 7),
    (7, 399458, 292996, 434517, 7, 45923, 49763, 7),
    (7, 101745, 7, 225606, 7, 156518, 201318, 7),
    (7, 306448, 7, 2679, 7, 32802, 421044, 7),
    (7, 7, 7, 424465, 7, 2167, 126117, 7),
    (7, 7, 7, 7, 7, 90706, 2135, 7),
    (7, 7, 7, 7, 7, 188998, 147574, 7),
    (7, 7, 7, 7, 7, 62131, 33041, 7),
    (7, 7, 7, 7, 7, 217766, 102658, 7),
    (7, 7, 7, 7, 7, 2071, 180486, 7),
    (7, 7, 7, 7, 7, 15381, 359536, 7),
    (7, 7, 7, 7, 7, 234326, 7, 7),
    (7, 7, 7, 7, 7, 322931, 7, 7),
    (7, 7, 7, 7, 7, 441701, 7, 7),
    (7, 7, 7, 7, 7, 213750, 7, 7),
    (7, 7, 7, 7, 7, 288821, 7, 7),
    (7, 7, 7, 7, 7, 237750, 7, 7),
    (7, 7, 7, 7, 7, 313428, 7, 7),
    (7, 7, 7, 7, 7, 250806, 7, 7),
    (7, 7, 7, 7, 7, 375796, 7, 7),
    (7, 7, 7, 7, 7, 343013, 7, 7),
    (7, 7, 7, 7, 7, 442672, 7, 7),
    (7, 7, 7, 7, 7, 119073, 7, 7),
    (7, 7, 7, 7, 7, 172326, 7, 7),
    (7, 7, 7, 7, 7, 180374, 7, 7),
    (7, 7, 7, 7, 7, 330325, 7, 7),
    (7, 7, 7, 7, 7, 335315, 7, 7),
    (7, 7, 7, 7, 7, 433362, 7, 7),
    (7, 7, 7, 7, 7, 2871, 7, 7),
    (7, 7, 7, 7, 7, 343475, 7, 7),
    (385973, 2199, 33091, 7, 70049, 41490, 462228, 217782),
    (246694, 2487, 7, 7, 33186, 258566, 69809, 254230),
    (306608, 77859, 7, 7, 82225, 2391, 176294, 49633),
    (127664, 2263, 7, 7, 164134, 314898, 7, 7),
    (471713, 306321, 7, 7, 160342, 325813, 7, 7),
    (58018, 380016, 7, 7, 295088, 425364, 7, 7),
    (209574, 7, 7, 7, 213158, 2263, 7, 7),
    (339090, 7, 7, 7, 7, 2967, 7, 7),
    (40960, 7, 7, 7, 7, 7, 7, 7),
    (277875, 326197, 2231, 7, 338229, 40993, 293204, 143510),
    (213718, 32081, 159990, 7, 301268, 7, 7, 301236),
    (7, 424113, 115667, 7, 288965, 7, 7, 7),
    (7, 305317, 164806, 7, 82162, 7, 7, 7),
    (7, 7, 7, 7, 205030, 7, 7, 7),
    (7, 2295, 404564, 309396, 110723, 2295, 331123, 309556),
    (7, 7, 93253, 330100, 314578, 426256, 62161, 7),
    (7, 7, 301268, 2647, 291696, 49409, 221894, 7),
    (7, 7, 7, 7, 62306, 123138, 298032, 7),
    (7, 7, 7, 7, 226150, 160006, 7, 7),
    (7, 7, 7, 7, 7, 65538, 7, 7),
    (319024, 2455, 294064, 310512, 412786, 164822, 213654, 147862),
    (164118, 176918, 305429, 94610, 2999, 455088, 363252, 213974),
    (281843, 102611, 309492, 53635, 2391, 86435, 293605, 321748),
    (340212, 123344, 107280, 237958, 321812, 225702, 2231, 338388),
    (286949, 151750, 168710, 58275, 354565, 2775, 335152, 197622),
    (168166, 225734, 94514, 318577, 98433, 7, 2263, 123761),
    (409043, 185270, 229670, 209622, 297460, 7, 301300, 115555),
    (7, 2391, 7, 205718, 349008, 7, 305381, 234342),
    (7, 383445, 7, 334036, 111425, 7, 318704, 346388),
    (7, 318546, 7, 411953, 238406, 7, 7, 185078),
    (7, 159990, 7, 7, 254966, 7, 7, 2423),
    (7, 445009, 7, 7, 2807, 7, 7, 73763),
    (7, 375365, 7, 7, 2455, 7, 7, 2295),
    (7, 164118, 7, 7, 385936, 7, 7, 7),
    (7, 7, 7, 7, 115585, 7, 7, 7),
    (7, 7, 7, 7, 197510, 7, 7, 7),
    (7, 7, 7, 7, 342260, 7, 7, 7),
    (7, 7, 7, 7, 297189, 7, 7, 7),
    (7, 7, 7, 7, 2935, 7, 7, 7),
    (86050, 7, 254230, 229750, 119059, 338708, 78593, 70577),
    (331376, 7, 53987, 342420, 168198, 78481, 242006, 250790),
    (184854, 7, 400437, 2391, 102530, 410244, 2327, 7),
    (332149, 7, 2391, 354740, 172374, 254598, 2359, 7),
    (176486, 7, 7, 54080, 188886, 433428, 69698, 7),
    (302387, 7, 7, 7, 7, 7, 412273, 7),
    (180566, 7, 7, 7, 7, 7, 7, 7),
    (7, 217430, 7, 127955, 338612, 98931, 7, 74033),
    (7, 2711, 7, 254918, 326309, 176742, 7, 172326),
    (7, 2359, 7, 7, 7, 366869, 7, 2679),
    (7, 310512, 7, 7, 7, 7, 7, 395600),
    (363795, 115376, 7, 404529, 314611, 372211, 185174, 7),
    (7, 66210, 7, 338979, 180598, 7, 7, 7),
    (7, 209574, 7, 189174, 7, 7, 7, 7),
    (7, 230294, 7, 2839, 7, 7, 7, 7),
    (7, 347536, 180790, 2519, 57379, 354612, 318004, 7),
    (7, 346997, 127011, 7, 7, 350613, 403856, 7),
    (7, 213398, 330100, 7, 7, 2423, 342404, 7),
    (7, 2423, 334325, 7, 7, 7, 375173, 7),
    (7, 7, 238006, 7, 7, 7, 246678, 7),
    (7, 7, 354740, 7, 7, 7, 2423, 7),
    (7, 7, 346533, 7, 7, 7, 7, 7),
    (7, 7, 193014, 7, 7, 7, 7, 7),
    (319989, 123315, 70096, 330896, 326068, 221590, 334357, 2455),
    (192998, 188838, 74179, 201270, 334245, 391669, 7, 94802),
    (327059, 2967, 213446, 7, 360944, 7, 7, 193094),
    (287156, 197622, 420369, 7, 192998, 7, 7, 2647),
    (344485, 7, 363012, 7, 347092, 7, 7, 121877),
    (197030, 7, 424881, 7, 351173, 7, 7, 7),
    (311860, 7, 359333, 7, 364960, 7, 7, 7),
    (201254, 7, 7, 7, 7, 7, 7, 7),
    (319956, 7, 7, 7, 7, 7, 7, 7),
    (373189, 7, 7, 7, 7, 7, 7, 7),
    (205254, 7, 7, 7, 7, 7, 7, 7),
    (77859, 358901, 7, 351251, 2519, 7, 7, 188854),
    (7, 7, 7, 2551, 7, 7, 7, 420721),
    (7, 7, 7, 2615, 7, 7, 7, 7),
    (7, 7, 7, 425040, 7, 7, 7, 7),
    (396372, 221814, 111218, 213590, 7, 119698, 358836, 205270),
    (380242, 2583, 90723, 7, 7, 230278, 350629, 7),
    (217718, 7, 209510, 7, 7, 205302, 254934, 7),
    (455313, 7, 197142, 7, 7, 2487, 197206, 7),
    (221830, 7, 7, 7, 7, 102946, 2519, 7),
    (7, 127856, 379765, 7, 2583, 383509, 371189, 99121),
    (7, 111458, 7, 7, 2615, 7, 7, 238374),
    (7, 234342, 7, 7, 7, 7, 7, 362996),
    (7, 7, 7, 7, 7, 7, 7, 94691),
    (110690, 246358, 259062, 222070, 2647, 2615, 205334, 221750),
    (7, 7, 2615, 98928, 412819, 432753, 209462, 2615),
    (7, 7, 355536, 217702, 367380, 379492, 78594, 2583),
    (7, 7, 371857, 367284, 371461, 387733, 363601, 359568),
    (7, 7, 7, 2711, 2679, 7, 7, 375937),
    (7, 7, 7, 392401, 7, 7, 7, 7),
    (348948, 2679, 371316, 7, 217782, 375952, 2647, 230006),
    (230150, 2775, 2647, 7, 355635, 7, 7, 371348),
    (7, 242390, 7, 7, 2711, 7, 7, 7),
    (127043, 7, 2711, 119795, 7, 7, 250806, 7),
    (323685, 7, 7, 234470, 7, 7, 2871, 7),
    (234294, 7, 7, 7, 7, 7, 7, 7),
    (238326, 258870, 7, 379604, 7, 2743, 7, 376051),
    (347632, 7, 7, 7, 7, 7, 7, 2743),
    (353140, 2807, 380144, 246550, 2871, 246774, 408209, 2775),
    (340837, 2839, 7, 2807, 127761, 2807, 387716, 2807),
    (242534, 7, 7, 115504, 230150, 123697, 234230, 246550),
    (7, 7, 7, 242470, 234294, 242470, 7, 2871),
    (7, 7, 7, 7, 2775, 7, 7, 2903),
    (7, 7, 7, 7, 242422, 7, 7, 7),
    (7, 392497, 383700, 2903, 250806, 7, 226102, 7),
    (7, 7, 2743, 7, 7, 7, 2743, 7),
    (7, 7, 127856, 7, 7, 7, 383700, 7),
    (7, 7, 242534, 7, 7, 7, 383685, 7),
    (7, 7, 2807, 7, 7, 7, 7, 7),
    (7, 7, 7, 388052, 7, 2903, 7, 7),
    (7, 7, 7, 2935, 7, 2935, 7, 7),
    (368708, 7, 7, 2967, 2903, 7, 7, 7),
    (7, 7, 7, 7, 125840, 7, 7, 7),
    (385940, 2903, 2839, 2999, 7, 7, 2839, 258966),
    (357253, 7, 2871, 7, 7, 7, 3063, 7),
    (250758, 7, 2903, 7, 7, 7, 7, 7),
    (102496, 7, 7, 7, 7, 7, 7, 7),
    (102499, 7, 7, 7, 7, 7, 7, 7),
    (7, 7, 250806, 7, 7, 7, 7, 2999),
    (102466, 2999, 7, 7, 7, 2999, 7, 7),
    (381028, 7, 7, 7, 7, 7, 7, 7),
    (7, 254934, 7, 7, 7, 3031, 2903, 7),
    (7, 7, 7, 7, 7, 7, 392117, 7),
    (7, 7, 7, 7, 7, 7, 2935, 7),
    (254934, 3063, 392305, 3063, 7, 7, 2967, 7),
    (7, 7, 2967, 7, 7, 7, 388053, 7),
    (7, 7, 7, 7, 7, 7, 259062, 7),
    (259062, 7, 3031, 7, 259030, 7, 7, 3031),
    (7, 7, 3063, 7, 7, 7, 7, 3063),
)
SEGMENTS = (83, 9, 5, 6, 19, 7, 4, 4, 8, 11, 4, 5, 4, 6, 3, 3, 2, 6, 5, 2, 2, 5, 1, 2, 3, 3, 0, 0, 2, 0, 0, 0, 0)
BLOCKS = (
    (803072, 407081, 298570, 232800, 139664, 295597, 47690, 758240),
    (297348, 108580, 198080, 37196, 1023284, 331874, 153827, 920811),
    (460134, 185346, 494133, 317890, 33261, 170236, 175317, 726225),
    (617635, 839516, 421861, 518335, 600963, 903001, 2615, 1028706),
    (583559, 1043950, 996584, 268722, 194007, 734123, 835437, 1009098),
    (1029743, 751878, 856441, 587516, 826187, 539231, 1028944, 880208),
    (1013076, 816651, 816851, 1003285, 916246, 56990, 315326, 657064),
    (748277, 610551, 679452, 545657, 640085, 806376, 815380, 325048),
)
OWN = ((0, 5, 10, 2, 3, 11, 9, 5), (1, 0, 0, 1, 1, 0, 2, 1), (2, 1, 1, 26, 4, 1, 6, 3), (3, 15, 23, 29, 13, 17, 24, 15))
PARTNERS = ((0, 2, 10, 5, 3, 5, 9, 11), (1, 1, 0, 0, 1, 1, 2, 0), (2, 26, 1, 1, 4, 3, 6, 1), (3, 29, 23, 15, 13, 15, 24, 17))
TRANSIT = 20
TI = 512

ROWS, COLS, RANK, HALF = 2048, 1024, 64, 1024
OTHER, COL_SLOT, TRANSIT_SLOT = 32, 64, 96
SLOTS = TRANSIT_SLOT + TRANSIT
NI = len(ITEMS)


def split(x):
    high = x.astype(BF16)
    return high, (x - high.astype(F32)).astype(BF16)


def kernel(
    trailing, factors, vectors, inverse, slots, acc,
    buf, right, wide, block_core, part, by_row, total, cores, known, table,
    local_sem, recv_sem, send_sem, own_send, row_send, row_recv, col_send, col_recv,
):
    r, c = lax.axis_index("row"), lax.axis_index("col")
    z, x, y, k = r // 2, (r % 2) * 2 + (c // 2) % 2, c // 4, c % 2
    flip = x // 2
    sx, sy = 1 - 2 * flip, 1 - 2 * k
    xc = x + flip * (3 - 2 * x)
    delta = (sy * (y - z) + 4) % 4
    kind = xc * 4 + delta
    diagonal = jnp.where(kind == 0, 1, 0)
    q = c // 2

    def device(x, y, z, k):
        return (z * 2 + x // 2, y * 4 + (x % 2) * 2 + k)

    partner = (r, q * 2 + 1 - k)
    row_peers = [((r + i) % 8, c) for i in range(1, 8)]
    col_peers = [(r, (c + 2 * i) % 16) for i in range(1, 8)]
    outer = device(3 - x, y, z, k)

    start_acc = pltpu.make_async_copy(trailing, acc, local_sem.at[4])
    start_acc.start()
    bits = [kind % 2 == 1, (kind // 2) % 2 == 1, kind // 4 == 1]

    def pick(row):
        pairs = [jnp.where(bits[0], I32(row[2 * a + 1]), I32(row[2 * a])) for a in range(4)]
        pairs = [jnp.where(bits[1], pairs[2 * a + 1], pairs[2 * a]) for a in range(2)]
        return jnp.where(bits[2], pairs[1], pairs[0])

    own = []
    for j in range(2):
        here = jnp.where(k == 0, pick(OWN[j]), pick(OWN[2 + j]))
        there = jnp.where(k == 0, pick(PARTNERS[j]), pick(PARTNERS[2 + j]))
        for h in range(2):
            src = factors.at[pl.ds(j * RANK, RANK), pl.ds(h * HALF, HALF)]
            other = jnp.where(k == h, 0, 1)
            slot = here + OTHER * other
            own.append((src, there + OTHER * (1 - other)))
            pltpu.make_async_copy(src, buf.at[slot], recv_sem.at[slot]).start()

    barrier = pltpu.get_barrier_semaphore()
    greeted = row_peers + col_peers + [outer, partner]
    for peer in greeted:
        pl.semaphore_signal(barrier, inc=1, device_id=peer, device_id_type=MESH)

    for i, row in enumerate(ITEMS):
        table[i] = pick(row)

    nt = (((1,), (1,)), ((), ()))
    blank = jnp.zeros((RANK, RANK * 8), F32)
    first = lax.dot_general(
        vectors[0], jnp.concatenate([inverse[0], blank], axis=0), nt,
        precision=lax.Precision.HIGHEST, preferred_element_type=F32,
    )
    second = lax.dot_general(
        vectors[1], jnp.concatenate([blank, inverse[1]], axis=0), nt,
        precision=lax.Precision.HIGHEST, preferred_element_type=F32,
    )
    blank = jnp.zeros((RANK, 2 * RANK), F32)
    part[...] = lax.dot_general(
        first, jnp.concatenate([first, blank], axis=0), nt,
        precision=lax.Precision.HIGHEST, preferred_element_type=F32,
    ) + lax.dot_general(
        second, jnp.concatenate([blank, second], axis=0), nt,
        precision=lax.Precision.HIGHEST, preferred_element_type=F32,
    )
    block_core[...] = jnp.zeros_like(block_core)

    pl.semaphore_wait(barrier, len(greeted))

    own_copies = []
    for i, (src, slot) in enumerate(own):
        copy = pltpu.make_async_remote_copy(
            src_ref=src, dst_ref=buf.at[slot], send_sem=own_send.at[i], recv_sem=recv_sem.at[slot],
            device_id=partner, device_id_type=MESH,
        )
        copy.start()
        own_copies.append(copy)

    def arrived(slot):
        pltpu.make_async_copy(buf.at[slot], buf.at[slot], recv_sem.at[slot]).wait()

    def panel_at(code):
        block = 2 * ((sy * (code % 4) + z + 4) % 4) + (code // 4 + flip) % 2
        return 4 * block + code // 8

    def send_of(i, word):
        way = word % 16
        src, dst = (word // 32) % 128, (word // 4096) % 128
        axis, turn = way // 2, 1 - 2 * (way % 2)
        dx = jnp.where(axis == 0, sx * turn, 0)
        dy = jnp.where(axis == 1, sy * turn, 0)
        dz = jnp.where(axis == 2, sy * turn, 0)
        dk = jnp.where(axis == 3, 1, 0)
        target = device((x + dx + 4) % 4, (y + dy + 4) % 4, (z + dz + 4) % 4, (k + dk) % 2)
        return src, pltpu.make_async_remote_copy(
            src_ref=buf.at[src], dst_ref=buf.at[dst], send_sem=send_sem.at[i],
            recv_sem=recv_sem.at[dst], device_id=target, device_id_type=MESH,
        )

    def pass_on(i, word):
        src, copy = send_of(i, word)

        @pl.when((word // 16) % 2 == 1)
        def _():
            arrived(src)

        @pl.when(word % 16 < 7)
        def _():
            copy.start()

    def moves(i, _):
        pass_on(i, table[i])
        return 0

    def sent(i, _):
        @pl.when(table[i] % 16 < 7)
        def _():
            pltpu.make_async_copy(buf.at[0], buf.at[0], send_sem.at[i]).wait()

        return 0

    def prepare(block):
        codes = pick(BLOCKS[block])
        for a in range(4):
            place = 4 * block + a
            arrived(OTHER + place)
            panel = panel_at((codes // (1 << (5 * a))) % 32)
            high, low = split(buf[jnp.where(diagonal == 1, place, COL_SLOT + place)])
            wide[pl.ds(a * RANK, RANK)] = high
            wide[pl.ds(256 + a * RANK, RANK)] = high
            wide[pl.ds(512 + a * RANK, RANK)] = low
            slot = slots[panel]
            pair = known[(slot // 2) % 2 * 8 + slot // 4]
            lane = lax.broadcasted_iota(I32, (RANK, 2 * RANK), 1) // RANK
            same = jnp.where(slot % 2 == a % 2, F32(1), F32(0))
            moved = pair * same + pltpu.roll(pair, RANK, axis=1) * (F32(1) - same)
            block_core[pl.ds(a * RANK, RANK), pl.ds((a // 2) * 128, 128)] = jnp.where(
                lane == a % 2, moved, F32(0)
            )
        high, low = split(block_core[...])
        scaled = jnp.dot(
            jnp.concatenate([high, low, high], axis=1), wide[...], preferred_element_type=F32
        )
        high, low = split(scaled)
        right[0:256] = high
        right[256:512] = high
        right[512:768] = low

    def tile_rows(j):
        h = k if j * TI < HALF else 1 - k
        return pl.ds(pl.multiple_of(h * HALF + (j * TI) % HALF, TI), TI)

    def tile(block, j):
        if j == 0:
            prepare(block)
        base = 4 * block + (0 if j * TI < HALF else OTHER)
        left = buf[base : base + 4, :, (j * TI) % HALF : (j * TI) % HALF + TI]
        high, low = split(left.reshape(256, TI))
        rows = tile_rows(j)
        acc[rows] = acc[rows] - lax.dot_general(
            jnp.concatenate([high, low, high], axis=0), right[...], (((0,), (0,)), ((), ())),
            preferred_element_type=F32,
        )

    mine = k * 8 + q
    row_copies = [
        pltpu.make_async_remote_copy(
            src_ref=part, dst_ref=by_row.at[6 - i], send_sem=row_send.at[i],
            recv_sem=row_recv.at[6 - i], device_id=peer, device_id_type=MESH,
        )
        for i, peer in enumerate(row_peers)
    ]
    keep = pltpu.make_async_copy(total, cores.at[mine], local_sem.at[5])
    col_copies = [
        pltpu.make_async_remote_copy(
            src_ref=total, dst_ref=cores.at[mine], send_sem=col_send.at[i],
            recv_sem=col_recv.at[i], device_id=peer, device_id_type=MESH,
        )
        for i, peer in enumerate(col_peers)
    ]
    half = cores.at[pl.ds(k * 8, 8)]
    exchange = pltpu.make_async_remote_copy(
        src_ref=half, dst_ref=half, send_sem=col_send.at[7], recv_sem=col_recv.at[7],
        device_id=partner, device_id_type=MESH,
    )
    settle = pltpu.make_async_copy(cores, known, local_sem.at[6])

    def give_share():
        for copy in row_copies:
            copy.start()

    def add_shares():
        for i in range(7):
            pltpu.make_async_copy(part, by_row.at[i], row_recv.at[i]).wait()
        summed = part[...]
        for i in range(7):
            summed = summed + by_row[i]
        total[...] = summed

    def give_total():
        keep.start()
        for copy in col_copies:
            copy.start()

    def give_half():
        keep.wait()
        for i in range(7):
            sender = k * 8 + (q + 7 - i) % 8
            pltpu.make_async_copy(total, cores.at[sender], col_recv.at[i]).wait()
        exchange.start()

    def take_half():
        exchange.wait_recv()
        settle.start()
        settle.wait()
        start_acc.wait()

    def opening(i, _):
        word = table[i]

        @pl.when(word % 16 < 8)
        def _():
            pass_on(i, word)

        for phase, action in enumerate((give_share, add_shares, give_total, give_half, take_half)):
            pl.when(word % 16 == 9 + phase)(action)
        return 0

    lax.fori_loop(0, SEGMENTS[0], opening, 0)
    tiles = ROWS // TI
    done = SEGMENTS[0]
    end = checked = 0
    for t, length in enumerate(SEGMENTS):
        end += length
        if end > done:
            lax.fori_loop(done, end, moves, 0)
            done = end
        if t in (4 * tiles, 7 * tiles):
            early = sum(SEGMENTS[: t - tiles])
            lax.fori_loop(checked, early, sent, 0)
            checked = early
        if t < 8 * tiles:
            tile(t // tiles, t % tiles)

    for copy in own_copies + row_copies + col_copies + [exchange]:
        copy.wait_send()

    lax.fori_loop(checked, NI, sent, 0)


def body(trailing, panel_factors, vectors_t, inverse_lower_factors, slot_of_panel):
    hbm = pl.BlockSpec(memory_space=pl.ANY)
    vmem = pl.BlockSpec(memory_space=pltpu.VMEM)
    dma = pltpu.SemaphoreType.DMA
    return pl.pallas_call(
        kernel,
        out_shape=pltpu.VMEM((ROWS, COLS), F32),
        in_specs=[hbm, hbm, vmem, vmem, pl.BlockSpec(memory_space=pltpu.SMEM)],
        out_specs=vmem,
        scratch_shapes=[
            pltpu.VMEM((SLOTS, RANK, HALF), F32),
            pltpu.VMEM((768, COLS), BF16),
            pltpu.VMEM((768, COLS), BF16),
            pltpu.VMEM((256, 256), F32),
            pltpu.VMEM((RANK, 2 * RANK), F32),
            pltpu.VMEM((7, RANK, 2 * RANK), F32),
            pltpu.VMEM((RANK, 2 * RANK), F32),
            pltpu.VMEM((16, RANK, 2 * RANK), F32),
            pltpu.VMEM((16, RANK, 2 * RANK), F32),
            pltpu.SMEM((NI,), I32),
            dma((7,)), dma((SLOTS,)), dma((NI,)), dma((4,)), dma((7,)), dma((7,)), dma((8,)), dma((8,)),
        ],
        compiler_params=pltpu.CompilerParams(
            collective_id=0, has_side_effects=True, vmem_limit_bytes=55 * 2**20
        ),
        name="update",
    )(trailing, panel_factors, vectors_t, inverse_lower_factors, slot_of_panel)


def solution(mesh):
    return jax.shard_map(
        body,
        mesh=mesh,
        in_specs=(
            P("row", "col"),
            P("col", "row"),
            P("col", None, None),
            P("col", "row", None),
            P(),
        ),
        out_specs=P("row", "col"),
        check_vma=False,
    )
```

time: 134 us -> 125 us (0.933)
  the two profiles are of different devices: /device:TPU:66 before, /device:TPU:26 now
where the time goes in v3:
time: 125 us; the launch traced here: 124 us
  Pallas kernels  120 us (96%)
  local copies, waits for them, and re-layouts  3.4 us (3%)
    pallas_call x1, Pallas kernels, body(): pl.pallas_call(kernel, out_shape=pltpu.VMEM((ROWS, COLS), F32), in_specs=...  120 us
    unnamed x1, local copies, waits for them, and re-layouts  3.4 us

profile of v3, /device:TPU:26, one launch (start us, length us, event | category | flops | bytes accessed | tf_op | source)
XLA Modules:
  0.0 123.9 jit_solution(18402963843786749331)
XLA Ops:
  0.0 120.5 %update.1 = f32[2048,1024]{1,0:T(8,128)S(1)} custom-call(f32[2048,1024]{1,0:T(8,128)} %trailing.1, f32[128,2048]{1,0:T(8,128)} %factors.1, f32[2,64,512]{2,1,0:T(8,128)} %vectors.1, f32[2,64,512]{2,1,0:T(8,128)} %inverse.1, s32[32]{0:T(128)} %slots.1), custom_call_target="tpu_custom_call" | custom-call | tf_op jit(solution)/shard_map/update/pallas_call | solution.py:512
  120.5 3.4 %copy.7 = f32[2048,1024]{1,0:T(8,128)} copy(f32[2048,1024]{1,0:T(8,128)S(1)} %update.1) | data formatting | bytes 16777216

commit v4 on v3

--- a/solution.py
+++ b/solution.py
@@ -10,233 +10,235 @@
 
 ITEMS = (
     (9, 9, 9, 9, 9, 9, 9, 9),
-    (8240, 24754, 16, 24656, 16497, 430096, 20561, 61489),
+    (8240, 24754, 16, 24656, 16497, 430096, 20561, 65585),
     (458769, 397476, 33106, 426049, 24674, 45426, 41267, 393397),
     (36866, 10, 10, 36914, 413748, 78179, 10, 10),
-    (262181, 57392, 4144, 10, 262288, 10, 102609, 430192),
-    (10, 74227, 20482, 86051, 10, 107057, 90179, 65634),
-    (3, 11, 11, 394069, 29107, 11, 11, 49251),
-    (266325, 12304, 58098, 11, 413733, 401956, 45250, 397813),
-    (11, 8496, 28882, 45555, 11, 286003, 49521, 11),
-    (64, 413988, 393412, 418277, 20513, 417060, 41314, 49362),
-    (265267, 131366, 139462, 139750, 404498, 434512, 151910, 16579),
-    (82224, 264213, 65570, 24850, 307824, 422096, 99091, 241862),
-    (467233, 110752, 37042, 429331, 156262, 82241, 65554, 281776),
-    (348453, 107346, 65699, 164102, 266320, 28866, 28675, 429220),
+    (262181, 61488, 4144, 10, 262288, 10, 106705, 430192),
+    (10, 74259, 20482, 86051, 10, 107057, 90179, 65634),
+    (3, 11, 11, 394069, 33203, 11, 11, 49251),
+    (266325, 12304, 58098, 11, 413733, 401956, 45250, 397845),
+    (11, 8496, 28882, 45587, 11, 286003, 49521, 11),
+    (64, 413988, 393412, 418309, 20513, 417060, 41314, 49362),
+    (265267, 131366, 139462, 139782, 404498, 434512, 151910, 16579),
+    (82224, 264213, 69666, 24850, 307824, 422096, 99091, 237766),
+    (467233, 106656, 45234, 429331, 156262, 82241, 69650, 281776),
+    (348453, 99154, 61603, 164102, 266320, 28866, 28675, 429220),
     (160038, 107331, 151718, 49218, 139334, 90435, 131078, 392498),
-    (446609, 181062, 430769, 16, 317460, 139462, 265488, 418032),
-    (16514, 268341, 144038, 16387, 321541, 168262, 397717, 82145),
-    (24707, 396304, 57664, 405509, 119313, 8193, 164230, 164070),
-    (147590, 12, 2071, 167942, 246278, 53714, 12, 12),
-    (278032, 414353, 12, 393396, 12, 184774, 90353, 426352),
-    (367634, 205446, 70003, 155814, 408626, 277680, 8418, 209254),
-    (365140, 277173, 205158, 91056, 404563, 273569, 159974, 12449),
-    (188998, 82402, 41778, 86850, 73762, 45409, 86066, 36898),
-    (12, 13, 95011, 12, 2231, 438992, 86051, 412723),
-    (291028, 438420, 234278, 415761, 278544, 70339, 135206, 13),
-    (155846, 155782, 13, 272388, 94210, 201414, 13, 272533),
-    (273587, 168470, 86752, 410069, 81923, 12, 20627, 86113),
-    (12466, 73810, 398164, 184774, 131078, 273488, 143494, 61459),
+    (446609, 168774, 430769, 16, 317460, 139462, 265488, 418064),
+    (16514, 268341, 144038, 16387, 325637, 168262, 397717, 82177),
+    (24707, 396304, 57664, 405509, 119313, 8193, 164230, 164102),
+    (147590, 12, 2071, 167942, 250374, 53746, 12, 12),
+    (278032, 414353, 12, 393396, 12, 184806, 90353, 426352),
+    (367634, 205446, 74099, 155814, 408626, 277680, 8418, 209254),
+    (365140, 277173, 209254, 78768, 404563, 273569, 159974, 12449),
+    (188998, 82434, 41810, 86850, 73762, 45409, 90162, 36898),
+    (12, 13, 99139, 12, 2231, 438992, 86051, 412723),
+    (291028, 438420, 238406, 415761, 278544, 74435, 135206, 13),
+    (155846, 155782, 13, 272388, 94210, 205510, 13, 272533),
+    (273587, 176630, 90848, 410069, 86019, 12, 20627, 86113),
+    (12466, 77906, 398100, 184774, 131078, 273488, 143494, 65555),
     (16547, 90179, 441651, 322356, 264564, 281665, 397748, 139270),
-    (151718, 421956, 185158, 13, 280933, 27716, 237990, 2487),
-    (302672, 192582, 310290, 115347, 363699, 420933, 277712, 53585),
+    (151718, 421956, 185094, 13, 280933, 27716, 246182, 2487),
+    (302672, 196678, 314386, 115347, 363699, 420933, 277712, 53585),
     (277714, 28675, 2103, 180870, 13, 110706, 314561, 168262),
     (13, 453812, 11537, 280820, 287120, 20579, 2071, 379984),
-    (462961, 119344, 437507, 147670, 176518, 147558, 49618, 416835),
-    (266276, 430628, 201110, 106736, 33489, 384339, 16835, 76869),
-    (226134, 420657, 78480, 159974, 221894, 437573, 188870, 421077),
-    (295316, 301861, 115330, 273584, 37074, 13, 286035, 20643),
-    (285810, 201254, 189062, 2103, 209094, 412113, 109716, 111314),
-    (172422, 12290, 284789, 65650, 66194, 268741, 408709, 180934),
-    (7, 41123, 297044, 176230, 17027, 107283, 127858, 2071),
-    (7, 404530, 147606, 432209, 152198, 209670, 172902, 160278),
-    (7, 284757, 221910, 61970, 268340, 131158, 94898, 82579),
-    (7, 367824, 155734, 258566, 264229, 429300, 53923, 225926),
-    (7, 426740, 408016, 289044, 3063, 114739, 217766, 326930),
-    (7, 442484, 317892, 58274, 45617, 392304, 2103, 152406),
-    (7, 172774, 24579, 286000, 201254, 314465, 2167, 272436),
-    (7, 147558, 176726, 123571, 2135, 31844, 28961, 405589),
+    (462961, 420657, 437507, 147670, 176518, 147558, 49618, 416835),
+    (266276, 301861, 197014, 102640, 33489, 376147, 16835, 72773),
+    (226134, 123472, 74384, 159974, 221894, 437573, 188870, 421077),
+    (295316, 430660, 111234, 273584, 37074, 13, 286035, 20643),
+    (285810, 193094, 189062, 2103, 209094, 412145, 113812, 107122),
+    (172422, 12290, 284789, 65650, 66194, 268773, 408709, 180838),
+    (7, 41123, 297044, 176230, 17027, 115475, 123762, 2071),
+    (7, 404530, 147606, 432209, 152198, 213766, 172902, 160310),
+    (7, 284757, 221910, 62002, 268340, 131158, 107218, 86707),
+    (7, 367824, 155734, 258598, 264229, 429300, 53955, 225958),
+    (7, 426772, 408016, 289044, 3063, 118835, 221894, 326930),
+    (7, 442484, 317892, 58274, 45649, 392304, 2103, 152374),
+    (7, 172806, 24579, 286000, 205382, 314465, 2167, 272436),
+    (7, 147558, 176758, 123571, 2135, 31844, 28961, 405589),
     (7, 36898, 399664, 172710, 276628, 32771, 37154, 155718),
-    (7, 401412, 330021, 99139, 268421, 280725, 193014, 425075),
+    (7, 401412, 334117, 103235, 268421, 280725, 197142, 425075),
     (7, 297941, 246678, 143510, 290067, 450800, 2199, 305940),
-    (7, 53619, 338325, 196918, 2167, 57571, 78019, 359317),
-    (7, 143718, 45170, 2231, 7, 196838, 445456, 284756),
-    (7, 428305, 217190, 250294, 7, 396338, 35845, 2167),
-    (7, 407665, 415889, 292980, 7, 447344, 74354, 7),
-    (7, 399458, 292996, 434517, 7, 45923, 49763, 7),
-    (7, 101745, 7, 225606, 7, 156518, 201318, 7),
-    (7, 306448, 7, 2679, 7, 32802, 421044, 7),
-    (7, 7, 7, 424465, 7, 2167, 126117, 7),
-    (7, 7, 7, 7, 7, 90706, 2135, 7),
+    (7, 53619, 338325, 192886, 2167, 57571, 78019, 359317),
+    (7, 143718, 49266, 2231, 7, 200934, 445456, 284756),
+    (7, 428305, 217190, 250294, 7, 396338, 31749, 2167),
+    (7, 407665, 415889, 292980, 7, 447312, 62034, 7),
+    (7, 399458, 292996, 434517, 7, 45891, 49731, 7),
+    (7, 93553, 7, 229702, 7, 156486, 193094, 7),
+    (7, 306448, 7, 424497, 7, 32802, 421044, 7),
+    (7, 7, 7, 2679, 7, 2167, 130213, 7),
+    (7, 7, 7, 7, 7, 82514, 2135, 7),
     (7, 7, 7, 7, 7, 188998, 147574, 7),
     (7, 7, 7, 7, 7, 62131, 33041, 7),
-    (7, 7, 7, 7, 7, 217766, 102658, 7),
+    (7, 7, 7, 7, 7, 221862, 94466, 7),
     (7, 7, 7, 7, 7, 2071, 180486, 7),
     (7, 7, 7, 7, 7, 15381, 359536, 7),
-    (7, 7, 7, 7, 7, 234326, 7, 7),
+    (7, 7, 7, 7, 7, 226166, 7, 7),
     (7, 7, 7, 7, 7, 322931, 7, 7),
     (7, 7, 7, 7, 7, 441701, 7, 7),
-    (7, 7, 7, 7, 7, 213750, 7, 7),
+    (7, 7, 7, 7, 7, 217846, 7, 7),
     (7, 7, 7, 7, 7, 288821, 7, 7),
-    (7, 7, 7, 7, 7, 237750, 7, 7),
+    (7, 7, 7, 7, 7, 233654, 7, 7),
     (7, 7, 7, 7, 7, 313428, 7, 7),
-    (7, 7, 7, 7, 7, 250806, 7, 7),
-    (7, 7, 7, 7, 7, 375796, 7, 7),
-    (7, 7, 7, 7, 7, 343013, 7, 7),
+    (7, 7, 7, 7, 7, 250838, 7, 7),
+    (7, 7, 7, 7, 7, 371700, 7, 7),
+    (7, 7, 7, 7, 7, 338917, 7, 7),
     (7, 7, 7, 7, 7, 442672, 7, 7),
     (7, 7, 7, 7, 7, 119073, 7, 7),
     (7, 7, 7, 7, 7, 172326, 7, 7),
     (7, 7, 7, 7, 7, 180374, 7, 7),
-    (7, 7, 7, 7, 7, 330325, 7, 7),
-    (7, 7, 7, 7, 7, 335315, 7, 7),
+    (7, 7, 7, 7, 7, 334421, 7, 7),
+    (7, 7, 7, 7, 7, 339411, 7, 7),
     (7, 7, 7, 7, 7, 433362, 7, 7),
     (7, 7, 7, 7, 7, 2871, 7, 7),
     (7, 7, 7, 7, 7, 343475, 7, 7),
-    (385973, 2199, 33091, 7, 70049, 41490, 462228, 217782),
-    (246694, 2487, 7, 7, 33186, 258566, 69809, 254230),
-    (306608, 77859, 7, 7, 82225, 2391, 176294, 49633),
+    (385973, 2199, 33091, 7, 70049, 41490, 462228, 217814),
+    (246694, 2487, 2231, 7, 33186, 254470, 65713, 250102),
+    (306608, 77859, 7, 7, 82225, 2391, 176294, 37377),
     (127664, 2263, 7, 7, 164134, 314898, 7, 7),
-    (471713, 306321, 7, 7, 160342, 325813, 7, 7),
+    (471713, 306321, 7, 7, 160310, 329909, 7, 7),
     (58018, 380016, 7, 7, 295088, 425364, 7, 7),
     (209574, 7, 7, 7, 213158, 2263, 7, 7),
-    (339090, 7, 7, 7, 7, 2967, 7, 7),
+    (334994, 7, 7, 7, 7, 2967, 7, 7),
     (40960, 7, 7, 7, 7, 7, 7, 7),
-    (277875, 326197, 2231, 7, 338229, 40993, 293204, 143510),
-    (213718, 32081, 159990, 7, 301268, 7, 7, 301236),
-    (7, 424113, 115667, 7, 288965, 7, 7, 7),
-    (7, 305317, 164806, 7, 82162, 7, 7, 7),
-    (7, 7, 7, 7, 205030, 7, 7, 7),
-    (7, 2295, 404564, 309396, 110723, 2295, 331123, 309556),
-    (7, 7, 93253, 330100, 314578, 426256, 62161, 7),
-    (7, 7, 301268, 2647, 291696, 49409, 221894, 7),
-    (7, 7, 7, 7, 62306, 123138, 298032, 7),
-    (7, 7, 7, 7, 226150, 160006, 7, 7),
-    (7, 7, 7, 7, 7, 65538, 7, 7),
-    (319024, 2455, 294064, 310512, 412786, 164822, 213654, 147862),
-    (164118, 176918, 305429, 94610, 2999, 455088, 363252, 213974),
-    (281843, 102611, 309492, 53635, 2391, 86435, 293605, 321748),
-    (340212, 123344, 107280, 237958, 321812, 225702, 2231, 338388),
-    (286949, 151750, 168710, 58275, 354565, 2775, 335152, 197622),
-    (168166, 225734, 94514, 318577, 98433, 7, 2263, 123761),
-    (409043, 185270, 229670, 209622, 297460, 7, 301300, 115555),
-    (7, 2391, 7, 205718, 349008, 7, 305381, 234342),
-    (7, 383445, 7, 334036, 111425, 7, 318704, 346388),
-    (7, 318546, 7, 411953, 238406, 7, 7, 185078),
-    (7, 159990, 7, 7, 254966, 7, 7, 2423),
-    (7, 445009, 7, 7, 2807, 7, 7, 73763),
-    (7, 375365, 7, 7, 2455, 7, 7, 2295),
-    (7, 164118, 7, 7, 385936, 7, 7, 7),
-    (7, 7, 7, 7, 115585, 7, 7, 7),
-    (7, 7, 7, 7, 197510, 7, 7, 7),
-    (7, 7, 7, 7, 342260, 7, 7, 7),
+    (277875, 32081, 159990, 7, 338229, 40993, 293204, 143510),
+    (213718, 424113, 115667, 7, 301268, 7, 7, 301236),
+    (7, 305317, 164806, 7, 288965, 7, 7, 7),
+    (7, 326229, 404564, 7, 82162, 7, 7, 7),
+    (7, 7, 97349, 7, 200934, 7, 7, 7),
+    (7, 7, 301268, 309396, 110723, 2295, 331123, 309556),
+    (7, 7, 7, 334228, 314578, 426256, 62097, 7),
+    (7, 7, 7, 7, 291664, 49409, 213638, 7),
+    (7, 7, 7, 7, 58178, 123138, 298032, 7),
+    (7, 7, 7, 7, 226118, 164102, 7, 7),
+    (7, 7, 7, 7, 7, 69634, 7, 7),
+    (319024, 2295, 294064, 2647, 412786, 160694, 217782, 147862),
+    (164118, 2455, 305429, 310512, 2935, 455088, 363252, 214006),
+    (281843, 180950, 309492, 94514, 2391, 86435, 297701, 321748),
+    (340212, 102611, 115504, 53539, 321812, 237990, 2231, 342484),
+    (286949, 119248, 168742, 237862, 354565, 2775, 326960, 197590),
+    (168166, 151750, 90418, 209654, 98433, 7, 2263, 127857),
+    (409043, 221638, 233766, 58275, 293364, 7, 301300, 107363),
+    (7, 185270, 7, 318577, 349072, 7, 305381, 234342),
+    (7, 318546, 7, 201590, 111489, 7, 318704, 350452),
+    (7, 2391, 7, 329940, 246662, 7, 74497, 185174),
+    (7, 383445, 7, 338228, 254966, 7, 7, 2423),
+    (7, 159990, 7, 7, 2807, 7, 7, 77859),
+    (7, 444977, 7, 7, 2455, 7, 7, 2327),
+    (7, 375333, 7, 7, 385968, 7, 7, 7),
+    (7, 164118, 7, 7, 115617, 7, 7, 7),
+    (7, 7, 7, 7, 197542, 7, 7, 7),
+    (7, 7, 7, 7, 346356, 7, 7, 7),
     (7, 7, 7, 7, 297189, 7, 7, 7),
-    (7, 7, 7, 7, 2935, 7, 7, 7),
-    (86050, 7, 254230, 229750, 119059, 338708, 78593, 70577),
-    (331376, 7, 53987, 342420, 168198, 78481, 242006, 250790),
-    (184854, 7, 400437, 2391, 102530, 410244, 2327, 7),
-    (332149, 7, 2391, 354740, 172374, 254598, 2359, 7),
-    (176486, 7, 7, 54080, 188886, 433428, 69698, 7),
-    (302387, 7, 7, 7, 7, 7, 412273, 7),
+    (7, 7, 7, 7, 2903, 7, 7, 7),
+    (86050, 7, 254230, 412017, 119059, 334612, 242006, 62385),
+    (331376, 7, 53987, 221590, 168198, 433428, 2327, 254886),
+    (184854, 7, 400437, 2391, 102530, 78481, 2359, 7),
+    (336245, 7, 2391, 354740, 172374, 410244, 73794, 7),
+    (176486, 7, 7, 54080, 188886, 258694, 412241, 7),
+    (310579, 7, 7, 7, 7, 7, 7, 7),
     (180566, 7, 7, 7, 7, 7, 7, 7),
-    (7, 217430, 7, 127955, 338612, 98931, 7, 74033),
-    (7, 2711, 7, 254918, 326309, 176742, 7, 172326),
-    (7, 2359, 7, 7, 7, 366869, 7, 2679),
-    (7, 310512, 7, 7, 7, 7, 7, 395600),
-    (363795, 115376, 7, 404529, 314611, 372211, 185174, 7),
-    (7, 66210, 7, 338979, 180598, 7, 7, 7),
-    (7, 209574, 7, 189174, 7, 7, 7, 7),
-    (7, 230294, 7, 2839, 7, 7, 7, 7),
-    (7, 347536, 180790, 2519, 57379, 354612, 318004, 7),
-    (7, 346997, 127011, 7, 7, 350613, 403856, 7),
-    (7, 213398, 330100, 7, 7, 2423, 342404, 7),
-    (7, 2423, 334325, 7, 7, 7, 375173, 7),
-    (7, 7, 238006, 7, 7, 7, 246678, 7),
-    (7, 7, 354740, 7, 7, 7, 2423, 7),
-    (7, 7, 346533, 7, 7, 7, 7, 7),
-    (7, 7, 193014, 7, 7, 7, 7, 7),
-    (319989, 123315, 70096, 330896, 326068, 221590, 334357, 2455),
-    (192998, 188838, 74179, 201270, 334245, 391669, 7, 94802),
-    (327059, 2967, 213446, 7, 360944, 7, 7, 193094),
-    (287156, 197622, 420369, 7, 192998, 7, 7, 2647),
-    (344485, 7, 363012, 7, 347092, 7, 7, 121877),
-    (197030, 7, 424881, 7, 351173, 7, 7, 7),
-    (311860, 7, 359333, 7, 364960, 7, 7, 7),
+    (7, 2359, 7, 127987, 326324, 103027, 185238, 74033),
+    (7, 217430, 7, 254950, 322213, 176742, 7, 172326),
+    (7, 2711, 7, 7, 7, 366869, 7, 2711),
+    (7, 310512, 7, 7, 7, 380403, 7, 395600),
+    (363795, 115376, 7, 404529, 314611, 7, 7, 7),
+    (7, 70306, 7, 343075, 180598, 7, 7, 7),
+    (7, 209574, 7, 189142, 7, 7, 7, 7),
+    (7, 230294, 7, 7, 7, 7, 7, 7),
+    (7, 347536, 180758, 2839, 57379, 354612, 317940, 7),
+    (7, 346997, 127011, 2519, 7, 2423, 403856, 7),
+    (7, 2423, 326004, 7, 7, 354709, 342404, 7),
+    (7, 213398, 326133, 7, 7, 7, 375173, 7),
+    (7, 7, 229814, 7, 7, 7, 238422, 7),
+    (7, 7, 7, 7, 7, 7, 2423, 7),
+    (319989, 123315, 358836, 334992, 330164, 209302, 338485, 2455),
+    (192998, 188838, 346533, 205302, 334245, 391637, 7, 113685),
+    (331155, 7, 193014, 7, 365040, 7, 7, 94706),
+    (287156, 7, 7, 7, 192998, 7, 7, 188902),
+    (344485, 7, 7, 7, 351188, 7, 7, 2551),
+    (197030, 7, 7, 7, 351173, 7, 7, 7),
+    (299572, 7, 7, 7, 360864, 7, 7, 7),
     (201254, 7, 7, 7, 7, 7, 7, 7),
     (319956, 7, 7, 7, 7, 7, 7, 7),
     (373189, 7, 7, 7, 7, 7, 7, 7),
     (205254, 7, 7, 7, 7, 7, 7, 7),
-    (77859, 358901, 7, 351251, 2519, 7, 7, 188854),
-    (7, 7, 7, 2551, 7, 7, 7, 420721),
-    (7, 7, 7, 2615, 7, 7, 7, 7),
-    (7, 7, 7, 425040, 7, 7, 7, 7),
-    (396372, 221814, 111218, 213590, 7, 119698, 358836, 205270),
-    (380242, 2583, 90723, 7, 7, 230278, 350629, 7),
-    (217718, 7, 209510, 7, 7, 205302, 254934, 7),
-    (455313, 7, 197142, 7, 7, 2487, 197206, 7),
-    (221830, 7, 7, 7, 7, 102946, 2519, 7),
-    (7, 127856, 379765, 7, 2583, 383509, 371189, 99121),
-    (7, 111458, 7, 7, 2615, 7, 7, 238374),
-    (7, 234342, 7, 7, 7, 7, 7, 362996),
-    (7, 7, 7, 7, 7, 7, 7, 94691),
-    (110690, 246358, 259062, 222070, 2647, 2615, 205334, 221750),
-    (7, 7, 2615, 98928, 412819, 432753, 209462, 2615),
-    (7, 7, 355536, 217702, 367380, 379492, 78594, 2583),
-    (7, 7, 371857, 367284, 371461, 387733, 363601, 359568),
-    (7, 7, 7, 2711, 2679, 7, 7, 375937),
-    (7, 7, 7, 392401, 7, 7, 7, 7),
-    (348948, 2679, 371316, 7, 217782, 375952, 2647, 230006),
-    (230150, 2775, 2647, 7, 355635, 7, 7, 371348),
-    (7, 242390, 7, 7, 2711, 7, 7, 7),
-    (127043, 7, 2711, 119795, 7, 7, 250806, 7),
-    (323685, 7, 7, 234470, 7, 7, 2871, 7),
-    (234294, 7, 7, 7, 7, 7, 7, 7),
-    (238326, 258870, 7, 379604, 7, 2743, 7, 376051),
-    (347632, 7, 7, 7, 7, 7, 7, 2743),
-    (353140, 2807, 380144, 246550, 2871, 246774, 408209, 2775),
-    (340837, 2839, 7, 2807, 127761, 2807, 387716, 2807),
-    (242534, 7, 7, 115504, 230150, 123697, 234230, 246550),
-    (7, 7, 7, 242470, 234294, 242470, 7, 2871),
-    (7, 7, 7, 7, 2775, 7, 7, 2903),
-    (7, 7, 7, 7, 242422, 7, 7, 7),
-    (7, 392497, 383700, 2903, 250806, 7, 226102, 7),
-    (7, 7, 2743, 7, 7, 7, 2743, 7),
-    (7, 7, 127856, 7, 7, 7, 383700, 7),
-    (7, 7, 242534, 7, 7, 7, 383685, 7),
-    (7, 7, 2807, 7, 7, 7, 7, 7),
-    (7, 7, 7, 388052, 7, 2903, 7, 7),
-    (7, 7, 7, 2935, 7, 2935, 7, 7),
-    (368708, 7, 7, 2967, 2903, 7, 7, 7),
-    (7, 7, 7, 7, 125840, 7, 7, 7),
-    (385940, 2903, 2839, 2999, 7, 7, 2839, 258966),
-    (357253, 7, 2871, 7, 7, 7, 3063, 7),
-    (250758, 7, 2903, 7, 7, 7, 7, 7),
-    (102496, 7, 7, 7, 7, 7, 7, 7),
+    (77859, 2967, 61904, 351251, 2519, 119698, 7, 192950),
+    (7, 201718, 70083, 2551, 7, 230278, 7, 420721),
+    (7, 7, 213446, 2583, 7, 7, 7, 7),
+    (7, 7, 420401, 7, 7, 7, 7, 7),
+    (7, 7, 354852, 7, 7, 7, 7, 7),
+    (7, 7, 424881, 7, 7, 7, 7, 7),
+    (7, 7, 355237, 7, 7, 7, 7, 7),
+    (396372, 358933, 7, 425040, 7, 192982, 358836, 205270),
+    (380242, 225910, 7, 213590, 7, 7, 354725, 7),
+    (217718, 2551, 7, 7, 7, 7, 254934, 7),
+    (455313, 7, 7, 7, 7, 7, 201334, 7),
+    (221830, 7, 7, 7, 7, 7, 2519, 7),
+    (7, 7, 7, 7, 7, 7, 205302, 7),
+    (7, 7, 7, 7, 7, 7, 367125, 7),
+    (7, 7, 7, 7, 2583, 102946, 7, 99057),
+    (7, 7, 7, 7, 2615, 2487, 7, 242406),
+    (7, 7, 7, 7, 2647, 383509, 7, 363028),
+    (110690, 242230, 115282, 98928, 343347, 2615, 209462, 94723),
+    (7, 127856, 94787, 217702, 359220, 432753, 82690, 221782),
+    (7, 111458, 205382, 371380, 375589, 383588, 367697, 2615),
+    (7, 234342, 201270, 226198, 2679, 387733, 7, 2647),
+    (7, 7, 375669, 2711, 7, 7, 7, 7),
+    (348948, 2807, 347344, 7, 412819, 371856, 2679, 7),
+    (230150, 2679, 259062, 7, 217782, 7, 250806, 7),
+    (7, 7, 7, 7, 2711, 7, 7, 7),
+    (122947, 246518, 2583, 388305, 7, 7, 2871, 230038),
+    (327781, 7, 371284, 119763, 7, 7, 7, 379572),
+    (234294, 7, 363665, 234438, 7, 7, 7, 2679),
+    (238326, 7, 2679, 7, 7, 2743, 7, 7),
+    (347632, 7, 7, 7, 7, 7, 7, 7),
+    (357236, 254774, 2711, 379636, 2839, 2807, 387732, 376051),
+    (340837, 2775, 371952, 2775, 127793, 246774, 383621, 371856),
+    (242534, 2839, 7, 246550, 234278, 123697, 226102, 380033),
+    (7, 7, 7, 115504, 230166, 242470, 408241, 2775),
+    (7, 7, 7, 242470, 2775, 7, 383652, 7),
+    (7, 7, 7, 7, 242550, 7, 7, 7),
+    (7, 7, 7, 7, 238326, 7, 7, 7),
+    (7, 392497, 7, 2903, 7, 2903, 2775, 246550),
+    (7, 7, 7, 7, 7, 7, 234230, 2807),
+    (7, 7, 383700, 388084, 7, 2935, 7, 2871),
+    (368708, 7, 2743, 2935, 2967, 7, 7, 2903),
+    (7, 7, 2807, 7, 125872, 7, 7, 7),
+    (7, 7, 127856, 7, 7, 7, 7, 7),
+    (7, 7, 242534, 7, 7, 7, 7, 7),
+    (390036, 2903, 2839, 2967, 7, 7, 2839, 258966),
+    (361349, 7, 2871, 2999, 7, 7, 2903, 7),
+    (250758, 7, 7, 7, 7, 7, 3063, 7),
+    (98400, 7, 7, 7, 7, 7, 7, 7),
     (102499, 7, 7, 7, 7, 7, 7, 7),
-    (7, 7, 250806, 7, 7, 7, 7, 2999),
-    (102466, 2999, 7, 7, 7, 2999, 7, 7),
-    (381028, 7, 7, 7, 7, 7, 7, 7),
-    (7, 254934, 7, 7, 7, 3031, 2903, 7),
-    (7, 7, 7, 7, 7, 7, 392117, 7),
-    (7, 7, 7, 7, 7, 7, 2935, 7),
-    (254934, 3063, 392305, 3063, 7, 7, 2967, 7),
-    (7, 7, 2967, 7, 7, 7, 388053, 7),
+    (7, 7, 2903, 7, 7, 2999, 7, 2999),
+    (7, 7, 7, 7, 7, 3031, 7, 7),
+    (102466, 2999, 7, 7, 7, 7, 2935, 7),
+    (381028, 259030, 7, 7, 7, 7, 7, 7),
+    (254934, 7, 7, 3031, 7, 7, 388021, 7),
     (7, 7, 7, 7, 7, 7, 259062, 7),
-    (259062, 7, 3031, 7, 259030, 7, 7, 3031),
-    (7, 7, 3063, 7, 7, 7, 7, 3063),
+    (7, 7, 7, 7, 7, 7, 2967, 7),
+    (7, 3063, 250806, 7, 7, 7, 392149, 7),
+    (7, 7, 392305, 7, 7, 7, 7, 7),
+    (7, 7, 2967, 7, 7, 7, 7, 3031),
+    (7, 7, 7, 7, 259030, 7, 7, 7),
+    (259062, 7, 3031, 7, 7, 7, 7, 3063),
+    (7, 7, 3063, 7, 7, 7, 7, 7),
 )
-SEGMENTS = (83, 9, 5, 6, 19, 7, 4, 4, 8, 11, 4, 5, 4, 6, 3, 3, 2, 6, 5, 2, 2, 5, 1, 2, 3, 3, 0, 0, 2, 0, 0, 0, 0)
+SEGMENTS = (83, 9, 5, 6, 19, 7, 4, 4, 6, 11, 7, 7, 3, 5, 3, 3, 2, 7, 2, 1, 4, 5, 2, 2, 3, 2, 1, 1, 2, 0, 0, 0, 0)
 BLOCKS = (
     (803072, 407081, 298570, 232800, 139664, 295597, 47690, 758240),
-    (297348, 108580, 198080, 37196, 1023284, 331874, 153827, 920811),
-    (460134, 185346, 494133, 317890, 33261, 170236, 175317, 726225),
-    (617635, 839516, 421861, 518335, 600963, 903001, 2615, 1028706),
-    (583559, 1043950, 996584, 268722, 194007, 734123, 835437, 1009098),
-    (1029743, 751878, 856441, 587516, 826187, 539231, 1028944, 880208),
-    (1013076, 816651, 816851, 1003285, 916246, 56990, 315326, 657064),
-    (748277, 610551, 679452, 545657, 640085, 806376, 815380, 325048),
+    (297348, 108580, 198080, 37196, 1023284, 331874, 153827, 560363),
+    (460134, 185346, 494133, 482274, 33261, 170236, 175317, 726236),
+    (617635, 479068, 421861, 452777, 600963, 585561, 887351, 832098),
+    (583559, 1032057, 456967, 268879, 179127, 734123, 517536, 899423),
+    (1029743, 994566, 856441, 968444, 826187, 539231, 1042956, 707102),
+    (1013076, 816662, 809597, 839445, 93912, 755358, 316350, 682024),
+    (748277, 610551, 679452, 672638, 640702, 802408, 815379, 959928),
 )
-OWN = ((0, 5, 10, 2, 3, 11, 9, 5), (1, 0, 0, 1, 1, 0, 2, 1), (2, 1, 1, 26, 4, 1, 6, 3), (3, 15, 23, 29, 13, 17, 24, 15))
-PARTNERS = ((0, 2, 10, 5, 3, 5, 9, 11), (1, 1, 0, 0, 1, 1, 2, 0), (2, 26, 1, 1, 4, 3, 6, 1), (3, 29, 23, 15, 13, 15, 24, 17))
+OWN = ((0, 5, 10, 2, 3, 11, 9, 5), (1, 0, 0, 1, 1, 0, 2, 1), (2, 1, 1, 26, 4, 1, 6, 3), (3, 16, 23, 29, 13, 17, 24, 16))
+PARTNERS = ((0, 2, 10, 5, 3, 5, 9, 11), (1, 1, 0, 0, 1, 1, 2, 0), (2, 26, 1, 1, 4, 3, 6, 1), (3, 29, 23, 16, 13, 16, 24, 17))
 TRANSIT = 20
 TI = 512
 

time: 125 us -> 123 us (0.984); the launches traced: 124 us -> 123 us
  no operation moved by 1% of the time
where the time goes in v4:
time: 123 us
  Pallas kernels  120 us (98%)
  local copies, waits for them, and re-layouts  3.4 us (3%)
    pallas_call x1, Pallas kernels, body(): pl.pallas_call(kernel, out_shape=pltpu.VMEM((ROWS, COLS), F32), in_specs=...  120 us
    unnamed x1, local copies, waits for them, and re-layouts  3.4 us

profile of v4, /device:TPU:26, one launch (start us, length us, event | category | flops | bytes accessed | tf_op | source)
XLA Modules:
  0.0 123.4 jit_solution(11013345233265514513)
XLA Ops:
  0.0 120.0 %update.1 = f32[2048,1024]{1,0:T(8,128)S(1)} custom-call(f32[2048,1024]{1,0:T(8,128)} %trailing.1, f32[128,2048]{1,0:T(8,128)} %factors.1, f32[2,64,512]{2,1,0:T(8,128)} %vectors.1, f32[2,64,512]{2,1,0:T(8,128)} %inverse.1, s32[32]{0:T(128)} %slots.1), custom_call_target="tpu_custom_call" | custom-call | tf_op jit(solution)/shard_map/update/pallas_call | solution.py:514
  120.0 3.4 %copy.7 = f32[2048,1024]{1,0:T(8,128)} copy(f32[2048,1024]{1,0:T(8,128)S(1)} %update.1) | data formatting | bytes 16777216
